TPU v7x, 32 devices: a whole 2x2x4 slice. The times are simulated.
32 devices in a mesh: group: 16 (over z, x, core), dom: 2 (over y).
Axes of the slice: x: 2, y: 2, z: 4, core: 2. Of those that a mesh axis runs over, the one named last changes fastest.
Arguments:
- state: float32 [4, 16, 15600], P(None, 'group', 'dom'), may hold values from -6 to 6
- mesh_vel: float32 [3, 16, 15600], P(None, 'group', 'dom'), may hold values from -6 to 6
- disp: float32 [3, 16, 15600], P(None, 'group', 'dom'), may hold values from -6 to 6
- elem_size: float32 [16, 8192], P('group', 'dom'), may hold values from 0.5 to 2
- live_slabs: int32 [16, 2], P('group', 'dom'), may hold values from 1 to 4
- trace_rows: int32 [16, 2, 4, 1024], P('group', 'dom'), may hold values from 0 to 7799, as said below
- penalty: float32 [16, 2, 4, 1024], P('group', 'dom'), may hold values from 1 to 4
Outputs:
- residual: float32 [4, 16, 15600], P(None, 'group', 'dom')
- new_disp: float32 [3, 16, 15600], P(None, 'group', 'dom')
Inputs may be any that keep to these rules, and one draw needn't show every extreme that they name: `trace_rows`: rows of the element block itself, on its faces where the second index is 0 or 9 or the third index is 0 or 129.
All inputs are finite; a program needn't handle non-finite values.
Results may differ from a plain program's by a relative error of at most 0.0003.
Values sent between devices are 32-bit elements; how exact they have to be, the bound alone decides.
A program may use at most 64 MiB of HBM per device.

v0:
```python
import math

import jax
import jax.numpy as jnp
from jax import lax
from jax.sharding import PartitionSpec as P

PA = 6
PB = 10
PC = 130
CP = 7800
EPS = 1024


time_step = 0.5
viscosity = 0.05


def from_behind(shard, axis, by):
    count = lax.axis_size(axis)
    pairs = [(i, i + by) for i in range(count) if 0 <= i + by < count]
    return lax.ppermute(shard, axis, pairs)


def padded_2(block, sides, width):
    for axis, dim in sides:
        count = lax.axis_size(axis)
        forward = [(i, i + 1) for i in range(count - 1)]
        backward = [(target, source) for source, target in forward]
        low = lax.ppermute(
            lax.slice_in_dim(block, block.shape[dim] - width, None, axis=dim), axis, forward
        )
        high = lax.ppermute(lax.slice_in_dim(block, 0, width, axis=dim), axis, backward)
        block = jnp.concatenate([low, block, high], axis=dim)
    return block


def basis_tables():
    points = jnp.array([0.5 - math.sqrt(0.15), 0.5, 0.5 + math.sqrt(0.15)], jnp.float32)
    gauss_weights = jnp.array([5.0 / 18.0, 8.0 / 18.0, 5.0 / 18.0], jnp.float32)
    column = points[:, None]
    values = jnp.concatenate(
        [(1.0 - column) ** 2 / 2.0, (1.0 + 2.0 * column - 2.0 * column**2) / 2.0, column**2 / 2.0],
        axis=1,
    )
    slopes = jnp.concatenate([column - 1.0, 1.0 - 2.0 * column, column], axis=1)

    def triple(along_a, along_b, along_c):
        return jnp.einsum("ia,jb,kc->ijkabc", along_a, along_b, along_c).reshape(27, 27)

    stacked = jnp.concatenate(
        [
            triple(values, values, values),
            triple(slopes, values, values),
            triple(values, slopes, values),
            triple(values, values, slopes),
        ],
        axis=0,
    )
    quad_weights = jnp.einsum("i,j,k->ijk", gauss_weights, gauss_weights, gauss_weights).reshape(27)
    return (stacked, quad_weights)


def element_terms(planes, mesh_planes, sizes):
    stacked, quad_weights = basis_tables()
    inner_b = PB - 2
    inner_c = PC - 2

    def gather_local(cp_block):
        return jnp.stack(
            [
                cp_block[
                    :, shift_a, shift_b : shift_b + inner_b, shift_c : shift_c + inner_c
                ].reshape(cp_block.shape[0], EPS)
                for shift_a in range(3)
                for shift_b in range(3)
                for shift_c in range(3)
            ],
            axis=0,
        )

    local_vals = gather_local(planes)
    local_mesh = gather_local(mesh_planes)
    at_points = jnp.dot(
        stacked,
        local_vals.reshape(27, 4 * EPS),
        precision=lax.Precision.HIGHEST,
        preferred_element_type=jnp.float32,
    ).reshape(4, 27, 4, EPS)
    mesh_points = jnp.dot(
        stacked[:27],
        local_mesh.reshape(27, 3 * EPS),
        precision=lax.Precision.HIGHEST,
        preferred_element_type=jnp.float32,
    ).reshape(27, 3, EPS)
    values_q = at_points[0]
    slopes_q = [at_points[1 + direction] / sizes for direction in range(3)]
    advect = values_q[:, :3] - mesh_points
    convect = (
        advect[:, 0:1] * slopes_q[0][:, :3]
        + advect[:, 1:2] * slopes_q[1][:, :3]
        + advect[:, 2:3] * slopes_q[2][:, :3]
    )
    momentum = convect + jnp.stack([slopes_q[component][:, 3] for component in range(3)], axis=1)
    continuity = slopes_q[0][:, 0] + slopes_q[1][:, 1] + slopes_q[2][:, 2]
    speed_sq = jnp.sum(advect * advect, axis=1)
    tau_moment = 1.0 / jnp.sqrt(
        4.0 / time_step**2 + 4.0 * speed_sq / sizes**2 + 36.0 * viscosity**2 / sizes**4
    )
    tau_contin = sizes**2 / (12.0 * tau_moment)
    pressure_part = values_q[:, 3] - tau_contin * continuity
    weight = quad_weights[:, None, None] * (sizes**3)[None, None, :]
    pieces = [weight * jnp.concatenate([convect, continuity[:, None]], axis=1)]
    for direction in range(3):
        unit_vector = (jnp.arange(3) == direction).astype(jnp.float32)
        velocity_part = (
            viscosity * slopes_q[direction][:, :3]
            + (advect[:, direction] * tau_moment)[:, None, :] * momentum
            - unit_vector[None, :, None] * pressure_part[:, None, :]
        )
        grad_coef = jnp.concatenate(
            [velocity_part, (tau_moment * momentum[:, direction])[:, None, :]], axis=1
        )
        pieces.append(weight * grad_coef / sizes)
    coefs = jnp.concatenate(pieces, axis=0)
    element_res = jnp.dot(
        stacked.T,
        coefs.reshape(108, 4 * EPS),
        precision=lax.Precision.HIGHEST,
        preferred_element_type=jnp.float32,
    ).reshape(27, 4, EPS)
    contrib = jnp.zeros((4, 3, PB, PC), jnp.float32)
    position = 0
    for shift_a in range(3):
        for shift_b in range(3):
            for shift_c in range(3):
                contrib = contrib.at[
                    :, shift_a, shift_b : shift_b + inner_b, shift_c : shift_c + inner_c
                ].add(element_res[position].reshape(4, inner_b, inner_c))
                position += 1
    return contrib


def block_residual(values, mesh_field, sizes, live_count):
    cp_grid = values.reshape(4, PA, PB, PC)
    mesh_grid = mesh_field.reshape(3, PA, PB, PC)

    def slab(slab_index, summed):
        planes = lax.dynamic_slice_in_dim(cp_grid, slab_index, 3, 1)
        mesh_planes = lax.dynamic_slice_in_dim(mesh_grid, slab_index, 3, 1)
        slab_sizes = lax.dynamic_slice_in_dim(sizes, slab_index * EPS, EPS)
        contrib = element_terms(planes, mesh_planes, slab_sizes)
        current = lax.dynamic_slice_in_dim(summed, slab_index, 3, 1)
        return lax.dynamic_update_slice_in_dim(summed, current + contrib, slab_index, 1)

    summed = lax.fori_loop(0, live_count, slab, jnp.zeros((4, PA, PB, PC), jnp.float32))
    return summed.reshape(4, PA, PB * PC)


def swap_traces(payload, offsets):
    received = []
    for which, step in enumerate(offsets):
        received.append(from_behind(payload[:, which ^ 1], "group", -step))
    return jnp.stack(received, axis=1)


def shards(state, mesh_vel, disp, elem_size, live_slabs, trace_rows, penalty):
    values = state[:, 0]
    mesh_field = mesh_vel[:, 0]
    moved = disp[:, 0] + 0.5 * mesh_field
    rows = trace_rows[0, 0]
    gammas = penalty[0, 0]
    local = block_residual(values, mesh_field, elem_size[0], live_slabs[0, 0])
    moved_planes = moved.reshape(3, PA, PB * PC)
    stacked_rims = jnp.concatenate([local, moved_planes], axis=0)
    dom_index = lax.axis_index("dom")
    has_prev = (dom_index > 0).astype(jnp.float32)
    has_next = (dom_index < lax.axis_size("dom") - 1).astype(jnp.float32)
    padded = padded_2(stacked_rims, (("dom", 1),), 2)
    before = padded[:, :2]
    after = padded[:, -2:]
    assembled = local.at[:, :2].add(before[:4]).at[:, -2:].add(after[:4])
    first_shift = has_prev * 0.5 * (before[4:] - moved_planes[:, :2])
    last_shift = has_next * 0.5 * (after[4:] - moved_planes[:, -2:])
    shared_shift = (
        jnp.zeros_like(moved_planes).at[:, :2].set(first_shift).at[:, -2:].set(last_shift)
    )
    assembled = assembled.reshape(4, CP)
    shared_shift = shared_shift.reshape(3, CP)
    group_count = lax.axis_size("group")
    group_index = lax.axis_index("group")
    stride = group_count // 2
    offsets = (1, -1, stride, -stride)
    present = jnp.stack(
        [(group_index + step >= 0) & (group_index + step < group_count) for step in offsets]
    )
    valid = present.astype(jnp.float32)
    flat_rows = rows.reshape(-1)
    payload = jnp.concatenate(
        [values[:, flat_rows], moved[:, flat_rows], assembled[:, flat_rows]], axis=0
    )
    payload = payload.reshape(11, 4, rows.shape[1])
    partner = swap_traces(payload, offsets)
    values_tr = payload[:4]
    moved_tr = payload[4:7]
    react_tr = payload[7:]
    values_par = partner[:4]
    moved_par = partner[4:7]
    react_par = partner[7:]
    mask = valid[None, :, None]
    term = mask * (gammas[None] * (values_tr - values_par) + 0.5 * (react_par - react_tr))
    residual = assembled.at[:, flat_rows].add(term.reshape(4, -1))
    slot_live = jnp.broadcast_to(present[:, None], rows.shape).astype(jnp.int32).reshape(-1)
    counted = jnp.zeros((CP,), jnp.int32).at[flat_rows].add(slot_live)
    disp_sum = (
        jnp.zeros((3, CP), jnp.float32)
        .at[:, flat_rows]
        .add((mask * (moved_par - moved_tr)).reshape(3, -1))
    )
    divisor = 2.0 * jnp.maximum(counted, 1).astype(jnp.float32)
    new_disp = moved + shared_shift + disp_sum / divisor[None, :]
    return (residual[:, None, :], new_disp[:, None, :])


def solution(mesh):
    return jax.shard_map(
        shards,
        mesh=mesh,
        in_specs=(
            P(None, "group", "dom"),
            P(None, "group", "dom"),
            P(None, "group", "dom"),
            P("group", "dom"),
            P("group", "dom"),
            P("group", "dom", None, None),
            P("group", "dom", None, None),
        ),
        out_specs=(P(None, "group", "dom"), P(None, "group", "dom")),
        check_vma=False,
    )
```

profile of v0, /device:TPU:0, one launch (start us, length us, event | category | flops | bytes accessed | tf_op | source)
XLA Modules:
  0.0 406.7 jit_solution(17151602158943359798)
XLA Ops:
  2.2 1.8 fusion.36
  6.6 246.2 %while.46 = (s32[]{:T(128)}, f32[4,6,10,130]{3,2,0,1:T(8,128)}, s32[]{:T(128)}, f32[4096]{0:T(1024)}, f32[4,6,10,130]{3,2,1,0:T(8,128)S(1)}, /*index=5*/f32[3,6,...) while((s32[]{:T(128)}, f32[4,6,10,130]{3,2,0,1:T(8,128)}, ...), condition=%wide.region_2.3_spmd.clone.clone, body=%wide.region_0.2_spmd.sunk.clone.clone.sunk | while | flops 319252480 | bytes 50661752 | solution.py:156
  14.1 1.8 constant_dynamic-slice_fusion.57
  18.3 1.6 fusion.64
  30.0 1.6 scatter-add.296
  34.0 1.6 scatter-add.299
  35.5 2.0 dynamic-slice_add_fusion.2
  37.5 3.5 scatter-add.300
  41.7 1.6 scatter-add.302
  43.4 1.6 scatter-add.303
  48.9 1.6 scatter-add.307
  50.6 1.6 scatter-add.308
  52.8 1.6 scatter-add.310
  54.5 1.6 scatter-add.311
  60.0 1.6 scatter-add.315
  61.7 1.6 scatter-add.316
  63.9 1.6 scatter-add.318
  65.6 1.6 scatter-add.319
  75.5 1.9 constant_dynamic-slice_fusion.57
  79.8 1.6 fusion.64
  91.4 1.6 scatter-add.296
  97.0 2.0 dynamic-slice_add_fusion.2
  98.9 3.5 scatter-add.300
  136.9 1.8 constant_dynamic-slice_fusion.57
  141.1 1.6 fusion.64
  152.8 1.6 scatter-add.296
  158.3 2.0 dynamic-slice_add_fusion.2
  160.3 3.5 scatter-add.300
  198.2 1.7 constant_dynamic-slice_fusion.57
  202.3 1.6 fusion.64
  214.0 1.6 scatter-add.296
  219.5 2.0 dynamic-slice_add_fusion.2
  221.5 3.5 scatter-add.300
  236.8 1.6 scatter-add.310
  256.1 4.6 %collective-permute-start = (f32[7,2,1300]{2,0,1:T(8,128)S(1)}, f32[7,2,1300]{2,0,1:T(8,128)S(1)}, u32[]{:S(2)}, u32[]{:S(2)}) collective-permute-start(f32[7,2,1300]{2,0,1:T(8,128)S(1)} %get-tuple-element.843), channel_id=1, source_target_pairs={{0,1},{2,3},{4,5},{6,7},{8,9},{10,11},{12,13},{14,15},{16,17},{18,... | collective-permute-start | bytes 218408 | tf_op jit(solution)/shard_map/ppermute | solution.py:30
  261.6 21.9 %scatter_custom_fusion.2 = s32[7800]{0:T(1024)S(1)} fusion(s32[4096]{0:T(1024)S(1)} %bitcast.590, s32[4096]{0:T(1024)S(1)} %bitcast.599, s32[]{:T(128)} %constant.1202.clone.1), kind=kCustom, calls=%fused_computation.191 | custom fusion | flops 4096 | bytes 31204 | tf_op jit(solution)/shard_map/scatter-add | solution.py:214
  283.6 3.4 copy.104
  287.1 2.8 copy.105
  289.9 12.9 %gather_fusion.1 = f32[4096,3]{1,0:T(8,128)S(1)} fusion(f32[3,7800]{0,1:T(8,128)} %copy.105, s32[4096]{0:T(1024)S(1)} %broadcast_clamp_fusion), kind=kCustom, calls=%fused_computation.1 | custom fusion | bytes 114688 | tf_op jit(solution)/shard_map/gather | solution.py:200
  304.0 12.9 %gather_fusion = f32[4096,4]{1,0:T(8,128)S(1)} fusion(f32[4,7800]{0,1:T(8,128)} %bitcast.503, s32[4096]{0:T(1024)S(1)} %broadcast_clamp_fusion), kind=kCustom, calls=%fused_computation | custom fusion | bytes 147456 | tf_op jit(solution)/shard_map/gather | solution.py:200
  318.5 2.8 copy.117
  321.3 12.9 %gather_fusion.2 = f32[4096,4]{1,0:T(8,128)S(1)} fusion(f32[4,7800]{0,1:T(8,128)} %copy.117, s32[4096]{0:T(1024)S(1)} %broadcast_clamp_fusion), kind=kCustom, calls=%fused_computation.2 | custom fusion | bytes 147456 | tf_op jit(solution)/shard_map/gather | solution.py:200
  335.2 5.4 %collective-permute-start.5 = (f32[11,1024]{1,0:T(8,128)S(1)}, f32[11,1024]{1,0:T(8,128)}, u32[]{:S(2)}, u32[]{:S(2)}) collective-permute-start(f32[11,1024]{1,0:T(8,128)S(1)} %bitcast.597), channel_id=1, source_target_pairs={{0,16},{2,18},{4,20},{6,22},{8,24},{10,26},{12,28},{14,30},{1,17},... | collective-permute-start | bytes 135176 | tf_op jit(solution)/shard_map/ppermute | solution.py:22
  346.4 2.7 collective-permute-done.4
  350.3 24.1 %scatter_fusion = f32[4,7800]{0,1:T(8,128)} fusion(f32[4,7800]{0,1:T(8,128)} %copy.117, s32[4096]{0:T(1024)S(1)} %bitcast.592, f32[4096,4]{1,0:T(8,128)S(1)} %bitcast.506), kind=kCustom, calls=%fused_computation.3 | custom fusion | flops 16384 | bytes 212992 | tf_op jit(solution)/shard_map/scatter-add | solution.py:212
  374.4 3.4 copy.124
  378.5 24.5 %scatter_custom_fusion.1 = f32[3,7800]{0,1:T(8,128)} fusion(s32[4096]{0:T(1024)S(1)} %bitcast.593, f32[4096,3]{1,0:T(8,128)S(1)} %bitcast.507, f32[]{:T(128)} %constant.1203.clone.1), kind=kCustom, calls=%fused_computation.157 | custom fusion | flops 12288 | bytes 93604 | tf_op jit(solution)/shard_map/scatter-add | solution.py:218
  403.0 2.9 copy.123
  (555 shorter events, 199.5 us)
Async XLA Ops:
  0.6 6.0 %copy-start.9 = (f32[3,3]{0,1:T(4,128)S(1)}, f32[3,3]{0,1:T(4,128)}, u32[]{:S(2)}) copy-start(f32[3,3]{0,1:T(4,128)} %constant.1442) | copy-start | bytes 112
  12.7 0.6 copy-start.3
  21.3 1.1 copy-start.4
  22.0 1.1 copy-start.6
  22.0 1.1 copy-start.7
  23.3 0.7 copy-start.13
  23.3 0.7 copy-start.14
  24.0 0.9 copy-start
  29.5 37.6 %copy-start.1 = (f32[4,6,10,130]{3,2,0,1:T(8,128)S(1)}, f32[4,6,10,130]{3,2,0,1:T(8,128)}, u32[]{:S(2)}) copy-start(f32[4,6,10,130]{3,2,0,1:T(8,128)} %get-tuple-element.1176) | copy-start | bytes 374404 | tf_op jit(solution)/shard_map/while
  29.5 38.4 %copy-start.10 = (f32[3,3]{0,1:T(4,128)S(1)}, f32[3,3]{0,1:T(4,128)}, u32[]{:S(2)}) copy-start(f32[3,3]{0,1:T(4,128)} %get-tuple-element.1235) | copy-start | bytes 112 | tf_op jit(solution)/shard_map/while
  67.2 0.7 copy-start.2
  82.7 1.1 copy-start.4
  83.4 1.1 copy-start.6
  83.5 1.1 copy-start.7
  84.8 0.7 copy-start.13
  84.8 0.7 copy-start.14
  85.4 0.9 copy-start
  90.9 37.6 %copy-start.1 = (f32[4,6,10,130]{3,2,0,1:T(8,128)S(1)}, f32[4,6,10,130]{3,2,0,1:T(8,128)}, u32[]{:S(2)}) copy-start(f32[4,6,10,130]{3,2,0,1:T(8,128)} %get-tuple-element.1176) | copy-start | bytes 374404 | tf_op jit(solution)/shard_map/while
  91.0 38.4 %copy-start.10 = (f32[3,3]{0,1:T(4,128)S(1)}, f32[3,3]{0,1:T(4,128)}, u32[]{:S(2)}) copy-start(f32[3,3]{0,1:T(4,128)} %get-tuple-element.1235) | copy-start | bytes 112 | tf_op jit(solution)/shard_map/while
  128.6 0.7 copy-start.2
  135.5 0.6 copy-start.3
  144.0 1.1 copy-start.4
  144.8 1.1 copy-start.6
  144.8 1.1 copy-start.7
  146.1 0.7 copy-start.13
  146.1 0.7 copy-start.14
  146.7 0.9 copy-start
  152.3 37.6 %copy-start.1 = (f32[4,6,10,130]{3,2,0,1:T(8,128)S(1)}, f32[4,6,10,130]{3,2,0,1:T(8,128)}, u32[]{:S(2)}) copy-start(f32[4,6,10,130]{3,2,0,1:T(8,128)} %get-tuple-element.1176) | copy-start | bytes 374404 | tf_op jit(solution)/shard_map/while
  152.3 38.4 %copy-start.10 = (f32[3,3]{0,1:T(4,128)S(1)}, f32[3,3]{0,1:T(4,128)}, u32[]{:S(2)}) copy-start(f32[3,3]{0,1:T(4,128)} %get-tuple-element.1235) | copy-start | bytes 112 | tf_op jit(solution)/shard_map/while
  190.0 0.7 copy-start.2
  205.2 1.1 copy-start.4
  206.0 1.1 copy-start.6
  206.0 1.1 copy-start.7
  207.3 0.7 copy-start.13
  207.3 0.7 copy-start.14
  207.9 0.9 copy-start
  213.5 37.6 %copy-start.1 = (f32[4,6,10,130]{3,2,0,1:T(8,128)S(1)}, f32[4,6,10,130]{3,2,0,1:T(8,128)}, u32[]{:S(2)}) copy-start(f32[4,6,10,130]{3,2,0,1:T(8,128)} %get-tuple-element.1176) | copy-start | bytes 374404 | tf_op jit(solution)/shard_map/while
  213.5 38.4 %copy-start.10 = (f32[3,3]{0,1:T(4,128)S(1)}, f32[3,3]{0,1:T(4,128)}, u32[]{:S(2)}) copy-start(f32[3,3]{0,1:T(4,128)} %get-tuple-element.1235) | copy-start | bytes 112 | tf_op jit(solution)/shard_map/while
  251.2 0.7 copy-start.2
  254.8 63.4 %collective-permute-start.1 = (f32[7,2,1300]{2,0,1:T(8,128)S(1)}, f32[7,2,1300]{2,0,1:T(8,128)S(1)}, u32[]{:S(2)}, u32[]{:S(2)}) collective-permute-start(f32[7,2,1300]{2,0,1:T(8,128)S(1)} %get-tuple-element.842), channel_id=1, source_target_pairs={{1,0},{3,2},{5,4},{7,6},{9,8},{11,10},{13,12},{15,14},{17,16},{19,... | collective-permute-start | bytes 218408 | tf_op jit(solution)/shard_map/ppermute | solution.py:33
  256.1 62.1 %collective-permute-start = (f32[7,2,1300]{2,0,1:T(8,128)S(1)}, f32[7,2,1300]{2,0,1:T(8,128)S(1)}, u32[]{:S(2)}, u32[]{:S(2)}) collective-permute-start(f32[7,2,1300]{2,0,1:T(8,128)S(1)} %get-tuple-element.843), channel_id=1, source_target_pairs={{0,1},{2,3},{4,5},{6,7},{8,9},{10,11},{12,13},{14,15},{16,17},{18,... | collective-permute-start | bytes 218408 | tf_op jit(solution)/shard_map/ppermute | solution.py:30
  283.6 3.5 copy-start.8
  316.9 1.5 copy-start.5
  335.2 14.4 %copy-start.11 = (f32[1,1,4,1024]{3,2,1,0:T(4,128)S(1)}, f32[1,1,4,1024]{3,2,1,0:T(4,128)}, u32[]{:S(2)}) copy-start(f32[1,1,4,1024]{3,2,1,0:T(4,128)} %param.79) | copy-start | bytes 49156
  335.2 10.2 %collective-permute-start.5 = (f32[11,1024]{1,0:T(8,128)S(1)}, f32[11,1024]{1,0:T(8,128)}, u32[]{:S(2)}, u32[]{:S(2)}) collective-permute-start(f32[11,1024]{1,0:T(8,128)S(1)} %bitcast.597), channel_id=1, source_target_pairs={{0,16},{2,18},{4,20},{6,22},{8,24},{10,26},{12,28},{14,30},{1,17},... | collective-permute-start | bytes 135176 | tf_op jit(solution)/shard_map/ppermute | solution.py:22
  340.7 5.6 %collective-permute-start.3 = (f32[11,1024]{1,0:T(8,128)S(1)}, f32[11,1024]{1,0:T(8,128)S(1)}, u32[]{:S(2)}, u32[]{:S(2)}) collective-permute-start(f32[11,1024]{1,0:T(8,128)S(1)} %bitcast.596), channel_id=1, source_target_pairs={{0,2},{2,4},{4,6},{6,8},{8,10},{10,12},{12,14},{14,16},{16,18},{18... | collective-permute-start | bytes 135176 | tf_op jit(solution)/shard_map/ppermute | solution.py:22
  342.0 7.1 %collective-permute-start.4 = (f32[11,1024]{1,0:T(8,128)S(1)}, f32[11,1024]{1,0:T(8,128)S(1)}, u32[]{:S(2)}, u32[]{:S(2)}) collective-permute-start(f32[11,1024]{1,0:T(8,128)S(1)} %bitcast.595), channel_id=1, source_target_pairs={{16,0},{18,2},{20,4},{22,6},{24,8},{26,10},{28,12},{30,14},{17,1},... | collective-permute-start | bytes 135176 | tf_op jit(solution)/shard_map/ppermute | solution.py:22
  343.3 6.0 %collective-permute-start.2 = (f32[11,1024]{1,0:T(8,128)S(1)}, f32[11,1024]{1,0:T(8,128)S(1)}, u32[]{:S(2)}, u32[]{:S(2)}) collective-permute-start(f32[11,1024]{1,0:T(8,128)S(1)} %bitcast.594), channel_id=1, source_target_pairs={{2,0},{4,2},{6,4},{8,6},{10,8},{12,10},{14,12},{16,14},{18,16},{20... | collective-permute-start | bytes 135176 | tf_op jit(solution)/shard_map/ppermute | solution.py:22
  (6 other events, 3.7 us)
where the time goes:
time: 409 us; the launch traced here: 407 us
  local copies, waits for them, and re-layouts  245 us (60%)
  other arithmetic  122 us (30%)
  starting transfers between devices  15.1 us (4%)
  matrix products  14.7 us (4%)
  loops' own time  6.23 us (2%)
    scatter-add x100, local copies, waits for them, and re-layouts, element_terms(): contrib = contrib.at[:, shift_a, shift_b:shift_b + inner_b, shift_c:shift...  135 us
    scatter-add x1, other arithmetic, shards(): disp_sum = jnp.zeros((3, CP), jnp.float32).at[:, flat_rows].add((mask * (...  24.5 us
    scatter-add x1, other arithmetic, shards(): residual = assembled.at[:, flat_rows].add(term.reshape(4, -1))  24.1 us
    scatter-add x1, other arithmetic, shards(): counted = jnp.zeros((CP,), jnp.int32).at[flat_rows].add(slot_live)  21.9 us
    gather x2, local copies, waits for them, and re-layouts, shards(): values[:, flat_rows]  13.5 us
    gather x2, local copies, waits for them, and re-layouts, shards(): moved[:, flat_rows]  13.5 us
    gather x2, local copies, waits for them, and re-layouts, shards(): assembled[:, flat_rows]  13.5 us
    while x128, local copies, waits for them, and re-layouts  13.4 us
  transfers between devices with their start and end apart: 6, of which 2 were waited for; matrix products, arithmetic and copies ran while one was open for 15% of the time, Pallas kernels for 0%

commit v1 on v0

v1 whole, which is shorter than its diff:
```python
import functools
import math

import jax
import jax.numpy as jnp
from jax import lax
from jax.experimental import pallas as pl
from jax.experimental.pallas import tpu as pltpu
from jax.sharding import PartitionSpec as P

PA = 6
PB = 10
PC = 130
CP = PA * PB * PC
SLABS = 4
ROWS = PA * PB
PLANE = PB * PC
LANES = 128
COLS = 61
WIDE = (COLS + 1) * LANES
SLOTS = 1024
SHARED = 2 * PLANE
RIM = 21 * LANES
LAST_COL = 4 * PLANE // LANES
LAST_OFF = 4 * PLANE % LANES
TABS = 14

DT = 0.5
NU = 0.05
S = math.sqrt(0.15)
W_EDGE = 5.0 / 18.0
W_MID = 8.0 / 18.0
F32 = jnp.float32
BF16 = jnp.bfloat16


def face_extras():
    out = []
    for a in range(PA):
        base = a * PLANE
        out += [base + b * PC + 129 for b in range(PB)]
        out += [base + 128, base + 9 * PC + 128]
        out += [base + b * PC for b in range(1, PB - 1)]
    return out


EXTRAS = face_extras()


def lane_iota():
    return lax.broadcasted_iota(jnp.int32, (8, LANES), 1)


def take_row(ref, start):
    off = start % LANES
    col = start - off
    first = ref[:, col : col + LANES]
    if off == 0:
        return first
    second = ref[:, col + LANES : col + 2 * LANES]
    mixed = jnp.where(lane_iota() >= off, first, second)
    return pltpu.roll(mixed, LANES - off, 1)


def add_row(ref, start, val):
    off = start % LANES
    col = start - off
    if off == 0:
        ref[:, col : col + LANES] += val
        return
    turned = pltpu.roll(val, off, 1)
    lane = lane_iota()
    ref[:, col : col + LANES] += jnp.where(lane >= off, turned, 0.0)
    ref[:, col + LANES : col + 2 * LANES] += jnp.where(lane < off, turned, 0.0)


def locate(row):
    plane = jnp.zeros_like(row)
    for k in range(1, PA):
        plane = plane + (row >= k * PLANE).astype(jnp.int32)
    rest = row - plane * PLANE
    along_b = jnp.zeros_like(row)
    for k in range(1, PB):
        along_b = along_b + (rest >= k * PC).astype(jnp.int32)
    along_c = rest - along_b * PC
    top = along_b == PB - 1
    straight = ((along_b == 0) | top) & (along_c < LANES)
    which = jnp.where(
        along_c == 129,
        along_b,
        jnp.where(along_c == 128, jnp.where(top, 11, 10), 11 + along_b),
    )
    hi = jnp.where(straight, 2 * plane + top.astype(jnp.int32), 12)
    lo = jnp.where(straight, along_c, 20 * plane + which)
    return hi, lo


def one_hot(lo):
    return (lax.broadcasted_iota(jnp.int32, (LANES, SLOTS), 0) == lo).astype(F32).astype(BF16)


def split_bf16(val):
    high = val.astype(BF16)
    low = (val - high.astype(F32)).astype(BF16)
    return high, low


def face_tables(x_ref, tab_ref):
    lane = lane_iota()
    for a in range(PA):
        tab_ref[16 * a : 16 * a + 8, :] = take_row(x_ref, a * PLANE)
        tab_ref[16 * a + 8 : 16 * a + 16, :] = take_row(x_ref, a * PLANE + 9 * PC)
    extra = jnp.zeros((8, LANES), F32)
    for k, flat in enumerate(EXTRAS):
        extra = jnp.where(lane == k, x_ref[:, flat : flat + 1], extra)
    tab_ref[96:104, :] = extra
    tab_ref[104:112, :] = jnp.zeros((8, LANES), F32)
    high, low = split_bf16(tab_ref[...])
    return jnp.concatenate([high, low], axis=0)


def gather_slots(table, hi, hot):
    full = jnp.dot(table, hot, preferred_element_type=F32)
    out = jnp.zeros((8, SLOTS), F32)
    for h in range(13):
        piece = full[8 * h : 8 * h + 8] + full[112 + 8 * h : 120 + 8 * h]
        out = jnp.where(hi == h, piece, out)
    return out


def trace_kernel(state_ref, mesh_ref, disp_ref, rows_ref, pay_ref, first_ref, last_ref, x_ref, tab_ref):
    for c in range(3):
        x_ref[c : c + 1, :CP] = disp_ref[c] + 0.5 * mesh_ref[c]
    x_ref[3:4, :CP] = jnp.zeros((1, CP), F32)
    for c in range(4):
        x_ref[4 + c : 5 + c, :CP] = state_ref[c]
    x_ref[:, COLS * LANES :] = jnp.zeros((8, LANES), F32)
    first_ref[...] = x_ref[0:4, :RIM]
    last_ref[...] = x_ref[0:4, LAST_COL * LANES : LAST_COL * LANES + RIM]
    table = face_tables(x_ref, tab_ref)
    for k in range(4):
        hi, lo = locate(rows_ref[k : k + 1, :])
        pay_ref[k] = gather_slots(table, hi, one_hot(lo))


def fwd_value(x0, x1, x2):
    even, odd = x0 + x2, x2 - x0
    base = 0.2 * even + 0.6 * x1
    mid = 0.125 * even + 0.75 * x1
    side = (S / 2) * odd
    return (base - side, mid, base + side)


def fwd_slope(x0, x1, x2):
    half = 0.5 * (x2 - x0)
    bend = S * ((x0 + x2) - 2.0 * x1)
    return (half - bend, half, half + bend)


def back_value(y0, y1, y2):
    even, odd = y0 + y2, y2 - y0
    ends = (W_EDGE * 0.2) * even + (W_MID * 0.125) * y1
    side = (W_EDGE * S / 2) * odd
    return (ends - side, (W_EDGE * 0.6) * even + (W_MID * 0.75) * y1, ends + side)


def back_slope(z0, z1, z2):
    turn = (W_EDGE * S) * (z2 - z0)
    half = (0.5 * W_EDGE) * (z0 + z2) + (0.5 * W_MID) * z1
    return (turn - half, -2.0 * turn, turn + half)


def both(value, slope):
    return tuple(v + d for v, d in zip(back_value(*value), back_slope(*slope)))


def strided(start):
    return pl.ds(start, 8, stride=8)


def element_kernel(
    live_ref, state_ref, mesh_ref, size_ref,
    out_ref, first_ref, last_ref,
    x_ref, q_ref, g_ref, acc_ref, h_ref,
):
    for c in range(4):
        x_ref[c : c + 1, :CP] = state_ref[c]
    for c in range(3):
        x_ref[4 + c : 5 + c, :CP] = state_ref[c] - mesh_ref[c]
    x_ref[7:8, :CP] = jnp.zeros((1, CP), F32)
    for k in range(32):
        h_ref[k // 8, k % 8 : k % 8 + 1, :] = size_ref[:, k * LANES : (k + 1) * LANES]
    for r in range(ROWS):
        taps = [take_row(x_ref, r * PC + s) for s in range(3)]
        for k, val in enumerate(fwd_value(*taps) + fwd_slope(*taps)):
            q_ref[k, 8 * r : 8 * r + 8, :] = val

    def along_b(a, carry):
        for f in range(7):
            for qc in range(3):
                value = [q_ref[qc, strided(a * 80 + 8 * s + f), :] for s in range(3)]
                if f >= 4:
                    for qb, val in enumerate(fwd_value(*value)):
                        g_ref[a, 3 * qb + qc, 8 + f] = val
                    continue
                slope = [q_ref[3 + qc, strided(a * 80 + 8 * s + f), :] for s in range(3)]
                vv = fwd_value(*value)
                dv = fwd_slope(*value)
                vd = fwd_value(*slope)
                for qb in range(3):
                    g_ref[a, 3 * qb + qc, 3 * f] = vv[qb]
                    g_ref[a, 3 * qb + qc, 3 * f + 1] = dv[qb]
                    g_ref[a, 3 * qb + qc, 3 * f + 2] = vd[qb]
        return carry

    lax.fori_loop(0, PA, along_b, 0)

    zero = jnp.zeros((8, LANES), F32)

    def clear(a, carry):
        for q in range(9):
            for k in range(12):
                acc_ref[a, q, k] = zero
        return carry

    lax.fori_loop(0, PA, clear, 0)

    def points(slab, q):
        h = h_ref[slab]

        def taps(slot):
            return [g_ref[slab + s, q, slot] for s in range(3)]

        grads = [
            [fwd_slope(*taps(3 * f)), fwd_value(*taps(3 * f + 1)), fwd_value(*taps(3 * f + 2))]
            for f in range(4)
        ]
        pressure = fwd_value(*taps(9))
        adv = [fwd_value(*taps(12 + c)) for c in range(3)]
        inv = 1.0 / h
        inv2 = inv * inv
        four = 4.0 * inv2
        fixed = 4.0 / DT**2 + (36.0 * NU**2) * (inv2 * inv2)
        h2 = (h * h) * (1.0 / 12.0)
        coef_f = [[None] * 3 for _ in range(4)]
        coef_k = [[[None] * 3 for _ in range(4)] for _ in range(3)]
        for t in range(3):
            a = [adv[c][t] for c in range(3)]
            conv = [
                a[0] * grads[c][0][t] + a[1] * grads[c][1][t] + a[2] * grads[c][2][t]
                for c in range(3)
            ]
            mom = [conv[c] + grads[3][c][t] for c in range(3)]
            cont = grads[0][0][t] + grads[1][1][t] + grads[2][2][t]
            total = fixed + four * (a[0] * a[0] + a[1] * a[1] + a[2] * a[2])
            tau = lax.rsqrt(total)
            press = h * pressure[t] - h2 * (total * tau) * cont
            scaled = [tau * mom[c] for c in range(3)]
            for c in range(3):
                coef_f[c][t] = h * conv[c]
                coef_k[c][3][t] = scaled[c]
                for d in range(3):
                    val = NU * grads[c][d][t] + a[d] * scaled[c]
                    coef_k[d][c][t] = val - press if d == c else val
            coef_f[3][t] = h * cont
        for c in range(4):
            parts = (
                both(coef_f[c], coef_k[0][c]),
                back_value(*coef_k[1][c]),
                back_value(*coef_k[2][c]),
            )
            for k, part in enumerate(parts):
                for s in range(3):
                    acc_ref[slab + s, q, 3 * c + k] += h * part[s]

    def slab_loop(slab, carry):
        def point_loop(q, inner):
            points(slab, q)
            return inner

        return lax.fori_loop(0, 9, point_loop, carry)

    lax.fori_loop(0, live_ref[0, 0], slab_loop, 0)

    def clear_rows(r, carry):
        for k in range(6):
            q_ref[k, pl.ds(pl.multiple_of(r * 8, 8), 8), :] = zero
        return carry

    lax.fori_loop(0, ROWS, clear_rows, 0)

    def back_b(a, carry):
        for c in range(4):
            for qc in range(3):
                pieces = [
                    [acc_ref[a, 3 * qb + qc, 3 * c + k] for qb in range(3)] for k in range(3)
                ]
                straight = both(pieces[0], pieces[1])
                sloped = back_value(*pieces[2])
                for s in range(3):
                    at = strided(a * 80 + 8 * s + 4 + c)
                    q_ref[qc, at, :] += straight[s]
                    q_ref[3 + qc, at, :] += sloped[s]
        return carry

    lax.fori_loop(0, PA, back_b, 0)

    lane = lane_iota()
    pending = zero
    for r in range(ROWS):
        y = [q_ref[k, 8 * r : 8 * r + 8, :] for k in range(6)]
        y0, y1, y2 = both(y[:3], y[3:])
        y1 = pltpu.roll(y1, 1, 1)
        y2 = pltpu.roll(y2, 2, 1)
        main = y0 + jnp.where(lane >= 1, y1, 0.0) + jnp.where(lane >= 2, y2, 0.0)
        tail = jnp.where(lane < 1, y1, 0.0) + jnp.where(lane < 2, y2, 0.0)
        off = 2 * r
        if off:
            main = pltpu.roll(main, off, 1)
            tail = pltpu.roll(tail, off, 1)
        out_ref[:, r * LANES : (r + 1) * LANES] = jnp.where(lane >= off, main, pending)
        pending = jnp.where(lane < off, main, tail)
    out_ref[:, ROWS * LANES : (ROWS + 1) * LANES] = pending
    out_ref[:, COLS * LANES :] = zero
    first_ref[...] = out_ref[4:8, :RIM]
    last_ref[...] = out_ref[4:8, LAST_COL * LANES : LAST_COL * LANES + RIM]


def rim_cut(col):
    return lane_iota() < min(LANES, SHARED - col * LANES)


def widen(rim_ref, wide_ref, low):
    wide_ref[...] = jnp.zeros_like(wide_ref)
    wide_ref[low : low + 4, :RIM] = rim_ref[...]


def assemble_kernel(local_ref, before_ref, after_ref, rows_ref, asm_ref, pay_ref, wide_ref, tab_ref):
    asm_ref[...] = local_ref[...]
    widen(before_ref, wide_ref, 4)
    for col in range(21):
        val = jnp.where(rim_cut(col), take_row(wide_ref, LAST_OFF + col * LANES), 0.0)
        asm_ref[:, col * LANES : (col + 1) * LANES] += val
    widen(after_ref, wide_ref, 4)
    for col in range(21):
        val = jnp.where(rim_cut(col), wide_ref[:, col * LANES : (col + 1) * LANES], 0.0)
        add_row(asm_ref, LAST_COL * LANES + LAST_OFF + col * LANES, val)
    table = face_tables(asm_ref, tab_ref)
    for k in range(4):
        hi, lo = locate(rows_ref[k : k + 1, :])
        pay_ref[k] = gather_slots(table, hi, one_hot(lo))[4:8]


def finish_kernel(
    flag_ref, asm_ref, mesh_ref, disp_ref, rows_ref, pen_ref,
    own_ref, own2_ref, p0_ref, p1_ref, p2_ref, p3_ref, r0_ref, r1_ref, r2_ref, r3_ref,
    before_ref, after_ref,
    res_ref, new_ref,
    x_ref, d_ref, wide_ref, term_ref,
):
    partners = (p0_ref, p1_ref, p2_ref, p3_ref)
    reactions = (r0_ref, r1_ref, r2_ref, r3_ref)
    acc = jnp.zeros((2 * 8 * TABS, LANES), F32)
    for k in range(4):
        live = flag_ref[0, k]
        gap = partners[k][...] - own_ref[k]
        term_ref[...] = gap * live
        term_ref[3:4, :] = jnp.zeros((1, SLOTS), F32) + live
        term_ref[4:8, :] = live * (
            0.5 * (reactions[k][...] - own2_ref[k]) - pen_ref[k : k + 1, :] * gap[4:8]
        )
        term = term_ref[...]
        hi, lo = locate(rows_ref[k : k + 1, :])
        hot = one_hot(lo)
        high = term.astype(BF16).astype(F32)
        low = term - high
        spread = [jnp.where(hi == h, high, 0.0) for h in range(TABS)]
        spread += [jnp.where(hi == h, low, 0.0) for h in range(TABS)]
        lhs = jnp.concatenate(spread, axis=0).astype(BF16)
        acc = acc + lax.dot_general(
            lhs, hot, (((1,), (1,)), ((), ())), preferred_element_type=F32
        )
    sums = acc[: 8 * TABS] + acc[8 * TABS :]
    d_ref[...] = jnp.zeros_like(d_ref)
    for a in range(PA):
        add_row(d_ref, a * PLANE, sums[16 * a : 16 * a + 8])
        add_row(d_ref, a * PLANE + 9 * PC, sums[16 * a + 8 : 16 * a + 16])
    lane = lane_iota()
    extra = sums[96:104]
    by_col = {}
    for k, flat in enumerate(EXTRAS):
        by_col.setdefault(flat // LANES, []).append((k, flat % LANES))
    for col, entries in by_col.items():
        val = d_ref[:, col * LANES : (col + 1) * LANES]
        for k, at in entries:
            val = val + jnp.where(lane == at, extra[:, k : k + 1], 0.0)
        d_ref[:, col * LANES : (col + 1) * LANES] = val

    for c in range(3):
        x_ref[c : c + 1, :CP] = disp_ref[c] + 0.5 * mesh_ref[c]
    x_ref[3:8, :CP] = jnp.zeros((5, CP), F32)
    x_ref[:, COLS * LANES :] = jnp.zeros((8, LANES), F32)
    top = lax.broadcasted_iota(jnp.int32, (8, LANES), 0) < 3
    for col in range(COLS):
        cut = slice(col * LANES, (col + 1) * LANES)
        d = d_ref[:, cut]
        averaged = d / (2.0 * jnp.maximum(d[3:4], 1.0))
        d_ref[:, cut] = jnp.where(top, averaged + x_ref[:, cut], d + asm_ref[:, cut])
    has_prev = 0.5 * flag_ref[0, 4]
    has_next = 0.5 * flag_ref[0, 5]
    widen(before_ref, wide_ref, 0)
    for col in range(21):
        cut = slice(col * LANES, (col + 1) * LANES)
        val = take_row(wide_ref, LAST_OFF + col * LANES) - x_ref[:, cut]
        d_ref[:, cut] += jnp.where(rim_cut(col) & top, has_prev * val, 0.0)
    widen(after_ref, wide_ref, 0)
    for col in range(21):
        start = LAST_COL * LANES + LAST_OFF + col * LANES
        val = wide_ref[:, col * LANES : (col + 1) * LANES] - take_row(x_ref, start)
        add_row(d_ref, start, jnp.where(rim_cut(col) & top, has_next * val, 0.0))
    for c in range(3):
        new_ref[c] = d_ref[c : c + 1, :CP]
    for c in range(4):
        res_ref[c] = d_ref[4 + c : 5 + c, :CP]


VMEM = pl.BlockSpec(memory_space=pltpu.VMEM)
SMEM = pl.BlockSpec(memory_space=pltpu.SMEM)


def shaped(*shape):
    return jax.ShapeDtypeStruct(shape, F32)


def cost(us):
    return pl.CostEstimate(flops=0, bytes_accessed=int(us * 3.0e6), transcendentals=0)


def call(kernel, outs, n_in, scratch, scalars=(), us=5):
    return pl.pallas_call(
        kernel,
        out_shape=outs,
        in_specs=[SMEM if k in scalars else VMEM for k in range(n_in)],
        out_specs=jax.tree.map(lambda _: VMEM, outs),
        scratch_shapes=[pltpu.VMEM(shape, F32) for shape in scratch],
        compiler_params=pltpu.CompilerParams(vmem_limit_bytes=48 << 20),
        cost_estimate=cost(us),
    )


def shift(shard, axis, by):
    count = lax.axis_size(axis)
    pairs = [(i, i + by) for i in range(count) if 0 <= i + by < count]
    return lax.ppermute(shard, axis, pairs)


def shards(state, mesh_vel, disp, elem_size, live_slabs, trace_rows, penalty):
    rows = trace_rows.reshape(4, SLOTS)
    gammas = penalty.reshape(4, SLOTS)
    groups = lax.axis_size("group")
    group = lax.axis_index("group")
    dom = lax.axis_index("dom")
    stride = groups // 2
    offsets = (1, -1, stride, -stride)
    flags = [(group + step >= 0) & (group + step < groups) for step in offsets]
    flags += [dom > 0, dom < lax.axis_size("dom") - 1, dom < 0, dom < 0]
    flags = jnp.stack(flags).astype(F32).reshape(1, 8)

    own, first, last = call(
        trace_kernel,
        (shaped(4, 8, SLOTS), shaped(4, RIM), shaped(4, RIM)),
        4,
        [(8, WIDE), (8 * TABS, LANES)],
        us=5,
    )(state, mesh_vel, disp, rows)
    partners = [shift(own[k ^ 1], "group", -step) for k, step in enumerate(offsets)]
    moved_before = shift(last, "dom", 1)
    moved_after = shift(first, "dom", -1)

    local, first, last = call(
        element_kernel,
        (shaped(8, WIDE), shaped(4, RIM), shaped(4, RIM)),
        4,
        [
            (8, WIDE),
            (6, 8 * ROWS, LANES),
            (PA, 9, 15, 8, LANES),
            (PA, 9, 12, 8, LANES),
            (SLABS, 8, LANES),
        ],
        scalars=(0,),
        us=15,
    )(live_slabs, state, mesh_vel, elem_size)
    before = shift(last, "dom", 1)
    after = shift(first, "dom", -1)
    assembled, own2 = call(
        assemble_kernel,
        (shaped(8, WIDE), shaped(4, 4, SLOTS)),
        4,
        [(8, RIM + LANES), (8 * TABS, LANES)],
        us=5,
    )(local, before, after, rows)
    reactions = [shift(own2[k ^ 1], "group", -step) for k, step in enumerate(offsets)]
    residual, new_disp = call(
        finish_kernel,
        (shaped(4, 1, CP), shaped(3, 1, CP)),
        18,
        [(8, WIDE), (8, WIDE), (8, RIM + LANES), (8, SLOTS)],
        scalars=(0,),
        us=8,
    )(flags, assembled, mesh_vel, disp, rows, gammas, own, own2, *partners, *reactions, moved_before, moved_after)
    return residual, new_disp


def solution(mesh):
    return jax.shard_map(
        shards,
        mesh=mesh,
        in_specs=(
            P(None, "group", "dom"),
            P(None, "group", "dom"),
            P(None, "group", "dom"),
            P("group", "dom"),
            P("group", "dom"),
            P("group", "dom", None, None),
            P("group", "dom", None, None),
        ),
        out_specs=(P(None, "group", "dom"), P(None, "group", "dom")),
        check_vma=False,
    )
```

time: 409 us -> 52.1 us (0.13)
  the two profiles are of different devices: /device:TPU:0 before, /device:TPU:31 now
where the time goes in v1:
time: 52.1 us; the launch traced here: 51.3 us
  starting transfers between devices  33.7 us (65%)
  Pallas kernels  9.46 us (18%)
  waiting for transfers between devices  3.93 us (8%)
  local copies, waits for them, and re-layouts  2.65 us (5%)
  between operations  1.55 us (3%)
    ppermute x12, starting transfers between devices, shift(): return lax.ppermute(shard, axis, pairs)  33.7 us
    pallas_call x1, Pallas kernels, shards(): call(element_kernel, (shaped(8, WIDE), shaped(4, RIM), shaped(4, RIM)), 4...  5.21 us
    ppermute x12, waiting for transfers between devices, shift(): return lax.ppermute(shard, axis, pairs)  3.93 us
    unnamed x14, local copies, waits for them, and re-layouts  2.52 us
    pallas_call x1, Pallas kernels, shards(): call(finish_kernel, (shaped(4, 1, CP), shaped(3, 1, CP)), 18, [(8, WIDE),...  2.39 us
  transfers between devices with their start and end apart: 12, of which 1 were waited for; matrix products, arithmetic and copies ran while one was open for 0% of the time, Pallas kernels for 4%

profile of v1, /device:TPU:31, one launch (start us, length us, event | category | flops | bytes accessed | tf_op | source)
XLA Modules:
  0.0 51.3 jit_solution(8276140635438733364)
XLA Ops:
  1.3 0.0 copy-start
  1.3 0.9 %copy-done = f32[3,1,7800]{2,1,0:T(1,128)S(1)} copy-done((f32[3,1,7800]{2,1,0:T(1,128)S(1)}, f32[3,1,7800]{2,1,0:T(1,128)}, u32[]{:S(2)}) %copy-start) | copy-done | bytes 93624
  2.2 0.0 copy-start.2
  2.2 0.9 %copy-done.2 = f32[4,1,7800]{2,1,0:T(1,128)S(1)} copy-done((f32[4,1,7800]{2,1,0:T(1,128)S(1)}, f32[4,1,7800]{2,1,0:T(1,128)}, u32[]{:S(2)}) %copy-start.2) | copy-done | bytes 124824
  3.1 0.0 copy-start.6
  3.1 0.7 %copy-done.6 = f32[1,4096]{1,0:T(1,128)S(1)} copy-done((f32[1,4096]{1,0:T(1,128)S(1)}, f32[1,4096]{1,0:T(1,128)}, u32[]{:S(2)}) %copy-start.6) | copy-done | bytes 16408
  3.8 0.0 copy-start.3
  3.8 0.0 copy-start.4
  3.8 5.2 %shard_map.86 = (f32[8,7936]{1,0:T(8,128)S(1)}, f32[4,2688]{1,0:T(4,128)S(1)}, f32[4,2688]{1,0:T(4,128)S(1)}) custom-call(s32[1,1]{1,0:T(1,128)S(6)} %copy.9.live_ref, f32[4,1,7800]{2,1,0:T(1,128)S(1)} %copy-done.2, f32[3,1,7800]{2,1,0:T(1,128)S(1)} %copy-done, f32[1,4096]{1,0:T(1,128)S(1)} %copy-done.6), custom_call_target="tpu_custom_call" | custom-call | bytes 45000000 | tf_op jit(solution)/shard_map/pallas_call | solution.py:480
  9.0 1.3 %collective-permute-start = (f32[4,2688]{1,0:T(4,128)S(1)}, f32[4,2688]{1,0:T(4,128)S(1)}, u32[]{:S(2)}, u32[]{:S(2)}) collective-permute-start(f32[4,2688]{1,0:T(4,128)S(1)} %get-tuple-element.11), channel_id=1, source_target_pairs={{0,1},{2,3},{4,5},{6,7},{8,9},{10,11},{12,13},{14,15},{16,17},{18,... | collective-permute-start | bytes 129032 | tf_op jit(solution)/shard_map/ppermute | solution.py:454
  10.3 4.0 %collective-permute-start.1 = (f32[4,2688]{1,0:T(4,128)S(1)}, f32[4,2688]{1,0:T(4,128)S(1)}, u32[]{:S(2)}, u32[]{:S(2)}) collective-permute-start(f32[4,2688]{1,0:T(4,128)S(1)} %get-tuple-element.12), channel_id=1, source_target_pairs={{1,0},{3,2},{5,4},{7,6},{9,8},{11,10},{13,12},{15,14},{17,16},{19,... | collective-permute-start | bytes 129032 | tf_op jit(solution)/shard_map/ppermute | solution.py:454
  14.3 0.0 copy-done.3
  14.3 0.0 copy-done.4
  14.3 0.9 %shard_map.88 = (f32[4,8,1024]{2,1,0:T(8,128)S(1)}, f32[4,2688]{1,0:T(4,128)S(1)}, f32[4,2688]{1,0:T(4,128)S(1)}) custom-call(f32[4,1,7800]{2,1,0:T(1,128)S(1)} %copy-done.2, f32[3,1,7800]{2,1,0:T(1,128)S(1)} %copy-done, f32[3,1,7800]{2,1,0:T(1,128)S(1)} %copy-done.3, s32[4,1024]{1,0:T(4,128)S(1)} %bitcast.25), custom_call_target="tpu_custom_call" | custom-call | bytes 15000000 | tf_op jit(solution)/shard_map/pallas_call | solution.py:469
  15.2 3.1 %collective-permute-start.2 = (f32[8,1024]{1,0:T(8,128)S(1)}, f32[8,1024]{1,0:T(8,128)S(1)}, u32[]{:S(2)}, u32[]{:S(2)}) collective-permute-start(f32[8,1024]{1,0:T(8,128)S(1)} %get-tuple-element.21), channel_id=1, source_target_pairs={{2,0},{4,2},{6,4},{8,6},{10,8},{12,10},{14,12},{16,14},{18,16},{20... | collective-permute-start | bytes 98312 | tf_op jit(solution)/shard_map/ppermute | solution.py:454
  18.4 1.3 %collective-permute-start.3 = (f32[8,1024]{1,0:T(8,128)S(1)}, f32[8,1024]{1,0:T(8,128)S(1)}, u32[]{:S(2)}, u32[]{:S(2)}) collective-permute-start(f32[8,1024]{1,0:T(8,128)S(1)} %get-tuple-element.20), channel_id=1, source_target_pairs={{0,2},{2,4},{4,6},{6,8},{8,10},{10,12},{12,14},{14,16},{16,18},{18... | collective-permute-start | bytes 98312 | tf_op jit(solution)/shard_map/ppermute | solution.py:454
  19.7 4.8 %collective-permute-start.4 = (f32[8,1024]{1,0:T(8,128)S(1)}, f32[8,1024]{1,0:T(8,128)S(1)}, u32[]{:S(2)}, u32[]{:S(2)}) collective-permute-start(f32[8,1024]{1,0:T(8,128)S(1)} %get-tuple-element.19), channel_id=1, source_target_pairs={{16,0},{18,2},{20,4},{22,6},{24,8},{26,10},{28,12},{30,14},{17,1},... | collective-permute-start | bytes 98312 | tf_op jit(solution)/shard_map/ppermute | solution.py:454
  24.5 0.0 collective-permute-done.before_ref
  24.5 1.3 %collective-permute-start.5 = (f32[8,1024]{1,0:T(8,128)S(1)}, f32[8,1024]{1,0:T(8,128)S(1)}, u32[]{:S(2)}, u32[]{:S(2)}) collective-permute-start(f32[8,1024]{1,0:T(8,128)S(1)} %get-tuple-element.18), channel_id=1, source_target_pairs={{0,16},{2,18},{4,20},{6,22},{8,24},{10,26},{12,28},{14,30},{1,17},... | collective-permute-start | bytes 98312 | tf_op jit(solution)/shard_map/ppermute | solution.py:454
  25.8 0.0 collective-permute-done.1.after_ref
  25.8 1.3 %collective-permute-start.10 = (f32[4,2688]{1,0:T(4,128)S(1)}, f32[4,2688]{1,0:T(4,128)S(1)}, u32[]{:S(2)}, u32[]{:S(2)}) collective-permute-start(f32[4,2688]{1,0:T(4,128)S(1)} %get-tuple-element.16), channel_id=1, source_target_pairs={{0,1},{2,3},{4,5},{6,7},{8,9},{10,11},{12,13},{14,15},{16,17},{18,... | collective-permute-start | bytes 129032 | tf_op jit(solution)/shard_map/ppermute | solution.py:454
  27.1 1.0 %shard_map.87 = (f32[8,7936]{1,0:T(8,128)S(1)}, f32[4,4,1024]{2,1,0:T(4,128)S(1)}) custom-call(f32[8,7936]{1,0:T(8,128)S(1)} %get-tuple-element.10.local_ref, f32[4,2688]{1,0:T(4,128)S(1)} %collective-permute-done.before_ref, f32[4,2688]{1,0:T(4,128)S(1)} %collective-permute-done.1.after_ref, s32[4,1024]{1,0:T(4,128)S(1)} %bitcast.26), custom_call_target="tpu_custom_call" | custom-call | bytes 15000000 | tf_op jit(solution)/shard_map/pallas_call | solution.py:496
  28.1 0.0 collective-permute-done.2.p0_ref
  28.1 4.0 %collective-permute-start.11 = (f32[4,2688]{1,0:T(4,128)S(1)}, f32[4,2688]{1,0:T(4,128)S(1)}, u32[]{:S(2)}, u32[]{:S(2)}) collective-permute-start(f32[4,2688]{1,0:T(4,128)S(1)} %get-tuple-element.17), channel_id=1, source_target_pairs={{1,0},{3,2},{5,4},{7,6},{9,8},{11,10},{13,12},{15,14},{17,16},{19,... | collective-permute-start | bytes 129032 | tf_op jit(solution)/shard_map/ppermute | solution.py:454
  32.1 0.0 copy-start.1
  32.1 0.0 collective-permute-done.3.p1_ref
  32.2 1.9 %collective-permute-start.6 = (f32[4,1024]{1,0:T(4,128)S(1)}, f32[4,1024]{1,0:T(4,128)S(1)}, u32[]{:S(2)}, u32[]{:S(2)}) collective-permute-start(f32[4,1024]{1,0:T(4,128)S(1)} %get-tuple-element.25), channel_id=1, source_target_pairs={{2,0},{4,2},{6,4},{8,6},{10,8},{12,10},{14,12},{16,14},{18,16},{20... | collective-permute-start | bytes 49160 | tf_op jit(solution)/shard_map/ppermute | solution.py:454
  34.0 0.0 collective-permute-done.4.p2_ref
  34.0 1.3 %collective-permute-start.7 = (f32[4,1024]{1,0:T(4,128)S(1)}, f32[4,1024]{1,0:T(4,128)S(1)}, u32[]{:S(2)}, u32[]{:S(2)}) collective-permute-start(f32[4,1024]{1,0:T(4,128)S(1)} %get-tuple-element.24), channel_id=1, source_target_pairs={{0,2},{2,4},{4,6},{6,8},{8,10},{10,12},{12,14},{14,16},{16,18},{18... | collective-permute-start | bytes 49160 | tf_op jit(solution)/shard_map/ppermute | solution.py:454
  35.3 0.0 collective-permute-done.5.p3_ref
  35.3 8.2 %collective-permute-start.8 = (f32[4,1024]{1,0:T(4,128)S(1)}, f32[4,1024]{1,0:T(4,128)S(1)}, u32[]{:S(2)}, u32[]{:S(2)}) collective-permute-start(f32[4,1024]{1,0:T(4,128)S(1)} %get-tuple-element.23), channel_id=1, source_target_pairs={{16,0},{18,2},{20,4},{22,6},{24,8},{26,10},{28,12},{30,14},{17,1},... | collective-permute-start | bytes 49160 | tf_op jit(solution)/shard_map/ppermute | solution.py:454
  43.6 0.0 collective-permute-done.10.before_ref
  43.6 1.3 %collective-permute-start.9 = (f32[4,1024]{1,0:T(4,128)S(1)}, f32[4,1024]{1,0:T(4,128)S(1)}, u32[]{:S(2)}, u32[]{:S(2)}) collective-permute-start(f32[4,1024]{1,0:T(4,128)S(1)} %get-tuple-element.22), channel_id=1, source_target_pairs={{0,16},{2,18},{4,20},{6,22},{8,24},{10,26},{12,28},{14,30},{1,17},... | collective-permute-start | bytes 49160 | tf_op jit(solution)/shard_map/ppermute | solution.py:454
  44.9 0.0 copy-start.5
  44.9 0.1 stack.32
  45.0 0.0 collective-permute-done.11.after_ref
  45.0 0.0 collective-permute-done.6.r0_ref
  45.0 0.0 collective-permute-done.7.r1_ref
  45.0 0.0 collective-permute-done.8.r2_ref
  45.0 3.9 %collective-permute-done.9.r3_ref = f32[4,1024]{1,0:T(4,128)S(1)} collective-permute-done((f32[4,1024]{1,0:T(4,128)S(1)}, f32[4,1024]{1,0:T(4,128)S(1)}, u32[]{:S(2)}, u32[]{:S(2)}) %collective-permute-start.9) | collective-permute-done | bytes 16416 | tf_op jit(solution)/shard_map/ppermute | solution.py:454
  48.9 0.0 copy-done.1
  49.0 0.0 copy-done.5
  49.0 2.4 %shard_map.89 = (f32[4,1,7800]{2,1,0:T(1,128)}, f32[3,1,7800]{2,1,0:T(1,128)}) custom-call(f32[1,8]{1,0:T(1,128)S(1)} %convert_element_type.10.flag_ref, f32[8,7936]{1,0:T(8,128)S(1)} %get-tuple-element.13.asm_ref, f32[3,1,7800]{2,1,0:T(1,128)S(1)} %copy-done.1, f32[3,1,7800]{2,1,0:T(1,128)S(1)} %copy-done.3, s32[4,1024]{1,0:T(4,128)S(1)} %bitcast.27, ...), custom_call_target="tpu_custom_call" | custom-call | bytes 24000000 | tf_op jit(solution)/shard_map/pallas_call | solution.py:504
  (3 shorter events, 0.0 us)
Async XLA Ops:
  1.3 0.9 %copy-start = (f32[3,1,7800]{2,1,0:T(1,128)S(1)}, f32[3,1,7800]{2,1,0:T(1,128)}, u32[]{:S(2)}) copy-start(f32[3,1,7800]{2,1,0:T(1,128)} %mesh_ref.5) | copy-start | bytes 280804
  2.2 0.9 %copy-start.2 = (f32[4,1,7800]{2,1,0:T(1,128)S(1)}, f32[4,1,7800]{2,1,0:T(1,128)}, u32[]{:S(2)}) copy-start(f32[4,1,7800]{2,1,0:T(1,128)} %state_ref.3) | copy-start | bytes 374404
  3.1 0.7 %copy-start.6 = (f32[1,4096]{1,0:T(1,128)S(1)}, f32[1,4096]{1,0:T(1,128)}, u32[]{:S(2)}) copy-start(f32[1,4096]{1,0:T(1,128)} %size_ref.1) | copy-start | bytes 49156
  3.8 10.5 %copy-start.3 = (f32[3,1,7800]{2,1,0:T(1,128)S(1)}, f32[3,1,7800]{2,1,0:T(1,128)}, u32[]{:S(2)}) copy-start(f32[3,1,7800]{2,1,0:T(1,128)} %disp_ref.3) | copy-start | bytes 280804
  3.8 10.5 %copy-start.4 = (s32[1,1,4,1024]{3,2,1,0:T(4,128)S(1)}, s32[1,1,4,1024]{3,2,1,0:T(4,128)}, u32[]{:S(2)}) copy-start(s32[1,1,4,1024]{3,2,1,0:T(4,128)} %param.12) | copy-start | bytes 49156
  9.0 15.5 %collective-permute-start = (f32[4,2688]{1,0:T(4,128)S(1)}, f32[4,2688]{1,0:T(4,128)S(1)}, u32[]{:S(2)}, u32[]{:S(2)}) collective-permute-start(f32[4,2688]{1,0:T(4,128)S(1)} %get-tuple-element.11), channel_id=1, source_target_pairs={{0,1},{2,3},{4,5},{6,7},{8,9},{10,11},{12,13},{14,15},{16,17},{18,... | collective-permute-start | bytes 129032 | tf_op jit(solution)/shard_map/ppermute | solution.py:454
  10.3 15.5 %collective-permute-start.1 = (f32[4,2688]{1,0:T(4,128)S(1)}, f32[4,2688]{1,0:T(4,128)S(1)}, u32[]{:S(2)}, u32[]{:S(2)}) collective-permute-start(f32[4,2688]{1,0:T(4,128)S(1)} %get-tuple-element.12), channel_id=1, source_target_pairs={{1,0},{3,2},{5,4},{7,6},{9,8},{11,10},{13,12},{15,14},{17,16},{19,... | collective-permute-start | bytes 129032 | tf_op jit(solution)/shard_map/ppermute | solution.py:454
  15.2 12.9 %collective-permute-start.2 = (f32[8,1024]{1,0:T(8,128)S(1)}, f32[8,1024]{1,0:T(8,128)S(1)}, u32[]{:S(2)}, u32[]{:S(2)}) collective-permute-start(f32[8,1024]{1,0:T(8,128)S(1)} %get-tuple-element.21), channel_id=1, source_target_pairs={{2,0},{4,2},{6,4},{8,6},{10,8},{12,10},{14,12},{16,14},{18,16},{20... | collective-permute-start | bytes 98312 | tf_op jit(solution)/shard_map/ppermute | solution.py:454
  18.4 13.8 %collective-permute-start.3 = (f32[8,1024]{1,0:T(8,128)S(1)}, f32[8,1024]{1,0:T(8,128)S(1)}, u32[]{:S(2)}, u32[]{:S(2)}) collective-permute-start(f32[8,1024]{1,0:T(8,128)S(1)} %get-tuple-element.20), channel_id=1, source_target_pairs={{0,2},{2,4},{4,6},{6,8},{8,10},{10,12},{12,14},{14,16},{16,18},{18... | collective-permute-start | bytes 98312 | tf_op jit(solution)/shard_map/ppermute | solution.py:454
  19.7 14.3 %collective-permute-start.4 = (f32[8,1024]{1,0:T(8,128)S(1)}, f32[8,1024]{1,0:T(8,128)S(1)}, u32[]{:S(2)}, u32[]{:S(2)}) collective-permute-start(f32[8,1024]{1,0:T(8,128)S(1)} %get-tuple-element.19), channel_id=1, source_target_pairs={{16,0},{18,2},{20,4},{22,6},{24,8},{26,10},{28,12},{30,14},{17,1},... | collective-permute-start | bytes 98312 | tf_op jit(solution)/shard_map/ppermute | solution.py:454
  24.5 10.8 %collective-permute-start.5 = (f32[8,1024]{1,0:T(8,128)S(1)}, f32[8,1024]{1,0:T(8,128)S(1)}, u32[]{:S(2)}, u32[]{:S(2)}) collective-permute-start(f32[8,1024]{1,0:T(8,128)S(1)} %get-tuple-element.18), channel_id=1, source_target_pairs={{0,16},{2,18},{4,20},{6,22},{8,24},{10,26},{12,28},{14,30},{1,17},... | collective-permute-start | bytes 98312 | tf_op jit(solution)/shard_map/ppermute | solution.py:454
  25.8 17.7 %collective-permute-start.10 = (f32[4,2688]{1,0:T(4,128)S(1)}, f32[4,2688]{1,0:T(4,128)S(1)}, u32[]{:S(2)}, u32[]{:S(2)}) collective-permute-start(f32[4,2688]{1,0:T(4,128)S(1)} %get-tuple-element.16), channel_id=1, source_target_pairs={{0,1},{2,3},{4,5},{6,7},{8,9},{10,11},{12,13},{14,15},{16,17},{18,... | collective-permute-start | bytes 129032 | tf_op jit(solution)/shard_map/ppermute | solution.py:454
  28.1 16.9 %collective-permute-start.11 = (f32[4,2688]{1,0:T(4,128)S(1)}, f32[4,2688]{1,0:T(4,128)S(1)}, u32[]{:S(2)}, u32[]{:S(2)}) collective-permute-start(f32[4,2688]{1,0:T(4,128)S(1)} %get-tuple-element.17), channel_id=1, source_target_pairs={{1,0},{3,2},{5,4},{7,6},{9,8},{11,10},{13,12},{15,14},{17,16},{19,... | collective-permute-start | bytes 129032 | tf_op jit(solution)/shard_map/ppermute | solution.py:454
  32.1 16.8 %copy-start.1 = (f32[3,1,7800]{2,1,0:T(1,128)S(1)}, f32[3,1,7800]{2,1,0:T(1,128)}, u32[]{:S(2)}) copy-start(f32[3,1,7800]{2,1,0:T(1,128)} %mesh_ref.5) | copy-start | bytes 280804
  32.2 12.9 %collective-permute-start.6 = (f32[4,1024]{1,0:T(4,128)S(1)}, f32[4,1024]{1,0:T(4,128)S(1)}, u32[]{:S(2)}, u32[]{:S(2)}) collective-permute-start(f32[4,1024]{1,0:T(4,128)S(1)} %get-tuple-element.25), channel_id=1, source_target_pairs={{2,0},{4,2},{6,4},{8,6},{10,8},{12,10},{14,12},{16,14},{18,16},{20... | collective-permute-start | bytes 49160 | tf_op jit(solution)/shard_map/ppermute | solution.py:454
  34.0 11.0 %collective-permute-start.7 = (f32[4,1024]{1,0:T(4,128)S(1)}, f32[4,1024]{1,0:T(4,128)S(1)}, u32[]{:S(2)}, u32[]{:S(2)}) collective-permute-start(f32[4,1024]{1,0:T(4,128)S(1)} %get-tuple-element.24), channel_id=1, source_target_pairs={{0,2},{2,4},{4,6},{6,8},{8,10},{10,12},{12,14},{14,16},{16,18},{18... | collective-permute-start | bytes 49160 | tf_op jit(solution)/shard_map/ppermute | solution.py:454
  35.3 9.7 %collective-permute-start.8 = (f32[4,1024]{1,0:T(4,128)S(1)}, f32[4,1024]{1,0:T(4,128)S(1)}, u32[]{:S(2)}, u32[]{:S(2)}) collective-permute-start(f32[4,1024]{1,0:T(4,128)S(1)} %get-tuple-element.23), channel_id=1, source_target_pairs={{16,0},{18,2},{20,4},{22,6},{24,8},{26,10},{28,12},{30,14},{17,1},... | collective-permute-start | bytes 49160 | tf_op jit(solution)/shard_map/ppermute | solution.py:454
  43.6 5.4 %collective-permute-start.9 = (f32[4,1024]{1,0:T(4,128)S(1)}, f32[4,1024]{1,0:T(4,128)S(1)}, u32[]{:S(2)}, u32[]{:S(2)}) collective-permute-start(f32[4,1024]{1,0:T(4,128)S(1)} %get-tuple-element.22), channel_id=1, source_target_pairs={{0,16},{2,18},{4,20},{6,22},{8,24},{10,26},{12,28},{14,30},{1,17},... | collective-permute-start | bytes 49160 | tf_op jit(solution)/shard_map/ppermute | solution.py:454
  44.9 4.1 %copy-start.5 = (f32[1,1,4,1024]{3,2,1,0:T(4,128)S(1)}, f32[1,1,4,1024]{3,2,1,0:T(4,128)}, u32[]{:S(2)}) copy-start(f32[1,1,4,1024]{3,2,1,0:T(4,128)} %param.13) | copy-start | bytes 49156

commit v2 on v1

--- a/solution.py
+++ b/solution.py
@@ -1,4 +1,3 @@
-import functools
 import math
 
 import jax
@@ -128,21 +127,6 @@
     return out
 
 
-def trace_kernel(state_ref, mesh_ref, disp_ref, rows_ref, pay_ref, first_ref, last_ref, x_ref, tab_ref):
-    for c in range(3):
-        x_ref[c : c + 1, :CP] = disp_ref[c] + 0.5 * mesh_ref[c]
-    x_ref[3:4, :CP] = jnp.zeros((1, CP), F32)
-    for c in range(4):
-        x_ref[4 + c : 5 + c, :CP] = state_ref[c]
-    x_ref[:, COLS * LANES :] = jnp.zeros((8, LANES), F32)
-    first_ref[...] = x_ref[0:4, :RIM]
-    last_ref[...] = x_ref[0:4, LAST_COL * LANES : LAST_COL * LANES + RIM]
-    table = face_tables(x_ref, tab_ref)
-    for k in range(4):
-        hi, lo = locate(rows_ref[k : k + 1, :])
-        pay_ref[k] = gather_slots(table, hi, one_hot(lo))
-
-
 def fwd_value(x0, x1, x2):
     even, odd = x0 + x2, x2 - x0
     base = 0.2 * even + 0.6 * x1
@@ -178,18 +162,7 @@
     return pl.ds(start, 8, stride=8)
 
 
-def element_kernel(
-    live_ref, state_ref, mesh_ref, size_ref,
-    out_ref, first_ref, last_ref,
-    x_ref, q_ref, g_ref, acc_ref, h_ref,
-):
-    for c in range(4):
-        x_ref[c : c + 1, :CP] = state_ref[c]
-    for c in range(3):
-        x_ref[4 + c : 5 + c, :CP] = state_ref[c] - mesh_ref[c]
-    x_ref[7:8, :CP] = jnp.zeros((1, CP), F32)
-    for k in range(32):
-        h_ref[k // 8, k % 8 : k % 8 + 1, :] = size_ref[:, k * LANES : (k + 1) * LANES]
+def element_stage(live, x_ref, q_ref, g_ref, acc_ref, h_ref, out_ref):
     for r in range(ROWS):
         taps = [take_row(x_ref, r * PC + s) for s in range(3)]
         for k, val in enumerate(fwd_value(*taps) + fwd_slope(*taps)):
@@ -227,6 +200,7 @@
 
     def points(slab, q):
         h = h_ref[slab]
+        outer = jnp.where(live > slab, h, 0.0)
 
         def taps(slot):
             return [g_ref[slab + s, q, slot] for s in range(3)]
@@ -271,7 +245,7 @@
             )
             for k, part in enumerate(parts):
                 for s in range(3):
-                    acc_ref[slab + s, q, 3 * c + k] += h * part[s]
+                    acc_ref[slab + s, q, 3 * c + k] += outer * part[s]
 
     def slab_loop(slab, carry):
         def point_loop(q, inner):
@@ -280,7 +254,7 @@
 
         return lax.fori_loop(0, 9, point_loop, carry)
 
-    lax.fori_loop(0, live_ref[0, 0], slab_loop, 0)
+    lax.fori_loop(0, SLABS, slab_loop, 0)
 
     def clear_rows(r, carry):
         for k in range(6):
@@ -322,8 +296,6 @@
         pending = jnp.where(lane < off, main, tail)
     out_ref[:, ROWS * LANES : (ROWS + 1) * LANES] = pending
     out_ref[:, COLS * LANES :] = zero
-    first_ref[...] = out_ref[4:8, :RIM]
-    last_ref[...] = out_ref[4:8, LAST_COL * LANES : LAST_COL * LANES + RIM]
 
 
 def rim_cut(col):
@@ -335,41 +307,194 @@
     wide_ref[low : low + 4, :RIM] = rim_ref[...]
 
 
-def assemble_kernel(local_ref, before_ref, after_ref, rows_ref, asm_ref, pay_ref, wide_ref, tab_ref):
-    asm_ref[...] = local_ref[...]
-    widen(before_ref, wide_ref, 4)
+def cut_rims(x_ref, low, rim_ref):
+    rim_ref[0] = x_ref[low : low + 4, :RIM]
+    rim_ref[1] = x_ref[low : low + 4, LAST_COL * LANES : LAST_COL * LANES + RIM]
+
+
+def main_kernel(
+    live_hbm, state_hbm, mesh_hbm, disp_hbm, size_hbm, rows_hbm, pen_hbm,
+    base_ref, term_ref,
+    live_ref, state_ref, mesh_ref, disp_ref, size_ref, rows_ref, pen_ref, x_ref, f_ref, q_ref, g_ref, acc_ref, h_ref, tab_ref, wide_ref,
+    own_ref, part_ref, own2_ref, part2_ref, rim_ref, rim_in_ref, rim2_ref, rim2_in_ref,
+    load_sem, send_sem, recv_sem,
+):
+    groups = lax.axis_size("group")
+    doms = lax.axis_size("dom")
+    group = lax.axis_index("group")
+    dom = lax.axis_index("dom")
+    stride = groups // 2
+    offsets = (1, -1, stride, -stride)
+    slots = [
+        (group + step, dom, (group + step >= 0) & (group + step < groups)) for step in offsets
+    ]
+    sides = [(group, dom - 1, dom > 0), (group, dom + 1, dom < doms - 1)]
+    loads = []
+    for src, dst, count in ((state_hbm, state_ref, 4), (mesh_hbm, mesh_ref, 3), (disp_hbm, disp_ref, 3)):
+        for c in range(count):
+            loads.append(
+                pltpu.make_async_copy(src.at[c], dst.at[c], load_sem.at[len(loads)])
+            )
+    small = (
+        (live_hbm, live_ref),
+        (size_hbm, size_ref),
+        (rows_hbm.at[0, 0], rows_ref),
+        (pen_hbm.at[0, 0], pen_ref),
+    )
+    for src, dst in small:
+        loads.append(pltpu.make_async_copy(src, dst, load_sem.at[len(loads)]))
+    for load in loads:
+        load.start()
+
+    barrier = pltpu.get_barrier_semaphore()
+    peers = 0
+    for to_group, to_dom, present in slots + sides:
+        peers = peers + present.astype(jnp.int32)
+
+        @pl.when(present)
+        def _():
+            pl.semaphore_signal(
+                barrier, inc=1, device_id=(to_group, to_dom), device_id_type=pl.DeviceIdType.MESH
+            )
+
+    def remote(src, dst, at, to, arrive):
+        return pltpu.make_async_remote_copy(
+            src_ref=src,
+            dst_ref=dst,
+            send_sem=send_sem.at[at],
+            recv_sem=recv_sem.at[arrive],
+            device_id=(to[0], to[1]),
+            device_id_type=pl.DeviceIdType.MESH,
+        )
+
+    def exchange(out_ref, in_ref, peers_of, sem):
+        return [
+            (to[2], remote(out_ref.at[k], in_ref.at[k ^ 1], sem + k, to, sem + (k ^ 1)),
+             remote(out_ref.at[k], in_ref.at[k], sem + k, to, sem + k))
+            for k, to in enumerate(peers_of)
+        ]
+
+    def launch(copies):
+        for present, out, _ in copies:
+
+            @pl.when(present)
+            def _():
+                out.start()
+
+    def land(copies):
+        for present, _, back in copies:
+
+            @pl.when(present)
+            def _():
+                back.wait_recv()
+
+    def drain(copies):
+        for present, out, _ in copies:
+
+            @pl.when(present)
+            def _():
+                out.wait_send()
+
+    traces = exchange(own_ref, part_ref, slots, 0)
+    traces2 = exchange(own2_ref, part2_ref, slots, 4)
+    rims = exchange(rim_ref, rim_in_ref, sides, 8)
+    rims2 = exchange(rim2_ref, rim2_in_ref, sides, 10)
+
+    for load in loads:
+        load.wait()
+    for c in range(3):
+        x_ref[c : c + 1, :CP] = disp_ref[c] + 0.5 * mesh_ref[c]
+        f_ref[4 + c : 5 + c, :CP] = state_ref[c] - mesh_ref[c]
+    x_ref[3:4, :CP] = jnp.zeros((1, CP), F32)
+    f_ref[7:8, :CP] = jnp.zeros((1, CP), F32)
+    for c in range(4):
+        x_ref[4 + c : 5 + c, :CP] = state_ref[c]
+        f_ref[c : c + 1, :CP] = state_ref[c]
+    x_ref[:, COLS * LANES :] = jnp.zeros((8, LANES), F32)
+    f_ref[:, COLS * LANES :] = jnp.zeros((8, LANES), F32)
+    for k in range(32):
+        h_ref[k // 8, k % 8 : k % 8 + 1, :] = size_ref[:, k * LANES : (k + 1) * LANES]
+    cut_rims(x_ref, 0, rim_ref)
+    table = face_tables(x_ref, tab_ref)
+    for k in range(4):
+        hi, lo = locate(rows_ref[k : k + 1, :])
+        own_ref[k] = gather_slots(table, hi, one_hot(lo))
+
+    pl.semaphore_wait(barrier, peers)
+    launch(rims)
+    launch(traces)
+
+    live = jnp.broadcast_to(live_ref[...], (8, LANES))
+    element_stage(live, f_ref, q_ref, g_ref, acc_ref, h_ref, base_ref)
+    cut_rims(base_ref, 4, rim2_ref)
+    launch(rims2)
+
+    for k, (_, _, present) in enumerate(slots):
+
+        @pl.when(jnp.logical_not(present))
+        def _():
+            part_ref[k] = jnp.zeros((8, SLOTS), F32)
+            part2_ref[k] = jnp.zeros((4, SLOTS), F32)
+
+    for k, (_, _, present) in enumerate(sides):
+
+        @pl.when(jnp.logical_not(present))
+        def _():
+            rim_in_ref[k] = jnp.zeros((4, RIM), F32)
+            rim2_in_ref[k] = jnp.zeros((4, RIM), F32)
+
+    land(rims)
+    has_prev = 0.5 * sides[0][2].astype(F32)
+    has_next = 0.5 * sides[1][2].astype(F32)
+    top = lax.broadcasted_iota(jnp.int32, (8, LANES), 0) < 3
+    for col in range(COLS):
+        cut = slice(col * LANES, (col + 1) * LANES)
+        base_ref[:, cut] = jnp.where(top, x_ref[:, cut], base_ref[:, cut])
+    widen(rim_in_ref.at[0], wide_ref, 0)
+    for col in range(21):
+        cut = slice(col * LANES, (col + 1) * LANES)
+        val = take_row(wide_ref, LAST_OFF + col * LANES) - x_ref[:, cut]
+        base_ref[:, cut] += jnp.where(rim_cut(col) & top, has_prev * val, 0.0)
+    widen(rim_in_ref.at[1], wide_ref, 0)
+    for col in range(21):
+        start = LAST_COL * LANES + LAST_OFF + col * LANES
+        val = wide_ref[:, col * LANES : (col + 1) * LANES] - take_row(x_ref, start)
+        add_row(base_ref, start, jnp.where(rim_cut(col) & top, has_next * val, 0.0))
+
+    land(rims2)
+    widen(rim2_in_ref.at[0], wide_ref, 4)
     for col in range(21):
         val = jnp.where(rim_cut(col), take_row(wide_ref, LAST_OFF + col * LANES), 0.0)
-        asm_ref[:, col * LANES : (col + 1) * LANES] += val
-    widen(after_ref, wide_ref, 4)
+        base_ref[:, col * LANES : (col + 1) * LANES] += val
+    widen(rim2_in_ref.at[1], wide_ref, 4)
     for col in range(21):
         val = jnp.where(rim_cut(col), wide_ref[:, col * LANES : (col + 1) * LANES], 0.0)
-        add_row(asm_ref, LAST_COL * LANES + LAST_OFF + col * LANES, val)
-    table = face_tables(asm_ref, tab_ref)
+        add_row(base_ref, LAST_COL * LANES + LAST_OFF + col * LANES, val)
+    table = face_tables(base_ref, tab_ref)
     for k in range(4):
         hi, lo = locate(rows_ref[k : k + 1, :])
-        pay_ref[k] = gather_slots(table, hi, one_hot(lo))[4:8]
-
-
-def finish_kernel(
-    flag_ref, asm_ref, mesh_ref, disp_ref, rows_ref, pen_ref,
-    own_ref, own2_ref, p0_ref, p1_ref, p2_ref, p3_ref, r0_ref, r1_ref, r2_ref, r3_ref,
-    before_ref, after_ref,
-    res_ref, new_ref,
-    x_ref, d_ref, wide_ref, term_ref,
-):
-    partners = (p0_ref, p1_ref, p2_ref, p3_ref)
-    reactions = (r0_ref, r1_ref, r2_ref, r3_ref)
+        own2_ref[k] = gather_slots(table, hi, one_hot(lo))[4:8]
+    launch(traces2)
+
+    land(traces)
+    for k, (_, _, present) in enumerate(slots):
+        live_slot = present.astype(F32)
+        gap = (part_ref[k] - own_ref[k]) * live_slot
+        term_ref[k] = gap
+        term_ref[k, 3:4, :] = jnp.zeros((1, SLOTS), F32) + live_slot
+        term_ref[k, 4:8, :] = -pen_ref[k : k + 1, :] * gap[4:8]
+    land(traces2)
+    for k, (_, _, present) in enumerate(slots):
+        half = 0.5 * present.astype(F32)
+        term_ref[k, 4:8, :] += half * (part2_ref[k] - own2_ref[k])
+    for copies in (rims, traces, rims2, traces2):
+        drain(copies)
+
+
+def finish_kernel(base_ref, term_in_ref, rows_ref, res_ref, new_ref, d_ref):
     acc = jnp.zeros((2 * 8 * TABS, LANES), F32)
     for k in range(4):
-        live = flag_ref[0, k]
-        gap = partners[k][...] - own_ref[k]
-        term_ref[...] = gap * live
-        term_ref[3:4, :] = jnp.zeros((1, SLOTS), F32) + live
-        term_ref[4:8, :] = live * (
-            0.5 * (reactions[k][...] - own2_ref[k]) - pen_ref[k : k + 1, :] * gap[4:8]
-        )
-        term = term_ref[...]
+        term = term_in_ref[k]
         hi, lo = locate(rows_ref[k : k + 1, :])
         hot = one_hot(lo)
         high = term.astype(BF16).astype(F32)
@@ -395,29 +520,12 @@
         for k, at in entries:
             val = val + jnp.where(lane == at, extra[:, k : k + 1], 0.0)
         d_ref[:, col * LANES : (col + 1) * LANES] = val
-
-    for c in range(3):
-        x_ref[c : c + 1, :CP] = disp_ref[c] + 0.5 * mesh_ref[c]
-    x_ref[3:8, :CP] = jnp.zeros((5, CP), F32)
-    x_ref[:, COLS * LANES :] = jnp.zeros((8, LANES), F32)
     top = lax.broadcasted_iota(jnp.int32, (8, LANES), 0) < 3
     for col in range(COLS):
         cut = slice(col * LANES, (col + 1) * LANES)
         d = d_ref[:, cut]
         averaged = d / (2.0 * jnp.maximum(d[3:4], 1.0))
-        d_ref[:, cut] = jnp.where(top, averaged + x_ref[:, cut], d + asm_ref[:, cut])
-    has_prev = 0.5 * flag_ref[0, 4]
-    has_next = 0.5 * flag_ref[0, 5]
-    widen(before_ref, wide_ref, 0)
-    for col in range(21):
-        cut = slice(col * LANES, (col + 1) * LANES)
-        val = take_row(wide_ref, LAST_OFF + col * LANES) - x_ref[:, cut]
-        d_ref[:, cut] += jnp.where(rim_cut(col) & top, has_prev * val, 0.0)
-    widen(after_ref, wide_ref, 0)
-    for col in range(21):
-        start = LAST_COL * LANES + LAST_OFF + col * LANES
-        val = wide_ref[:, col * LANES : (col + 1) * LANES] - take_row(x_ref, start)
-        add_row(d_ref, start, jnp.where(rim_cut(col) & top, has_next * val, 0.0))
+        d_ref[:, cut] = jnp.where(top, averaged, d) + base_ref[:, cut]
     for c in range(3):
         new_ref[c] = d_ref[c : c + 1, :CP]
     for c in range(4):
@@ -425,91 +533,60 @@
 
 
 VMEM = pl.BlockSpec(memory_space=pltpu.VMEM)
-SMEM = pl.BlockSpec(memory_space=pltpu.SMEM)
+HBM = pl.BlockSpec(memory_space=pltpu.HBM)
 
 
 def shaped(*shape):
     return jax.ShapeDtypeStruct(shape, F32)
 
 
-def cost(us):
-    return pl.CostEstimate(flops=0, bytes_accessed=int(us * 3.0e6), transcendentals=0)
-
-
-def call(kernel, outs, n_in, scratch, scalars=(), us=5):
-    return pl.pallas_call(
-        kernel,
-        out_shape=outs,
-        in_specs=[SMEM if k in scalars else VMEM for k in range(n_in)],
-        out_specs=jax.tree.map(lambda _: VMEM, outs),
-        scratch_shapes=[pltpu.VMEM(shape, F32) for shape in scratch],
-        compiler_params=pltpu.CompilerParams(vmem_limit_bytes=48 << 20),
-        cost_estimate=cost(us),
-    )
-
-
-def shift(shard, axis, by):
-    count = lax.axis_size(axis)
-    pairs = [(i, i + by) for i in range(count) if 0 <= i + by < count]
-    return lax.ppermute(shard, axis, pairs)
-
-
 def shards(state, mesh_vel, disp, elem_size, live_slabs, trace_rows, penalty):
     rows = trace_rows.reshape(4, SLOTS)
-    gammas = penalty.reshape(4, SLOTS)
-    groups = lax.axis_size("group")
-    group = lax.axis_index("group")
-    dom = lax.axis_index("dom")
-    stride = groups // 2
-    offsets = (1, -1, stride, -stride)
-    flags = [(group + step >= 0) & (group + step < groups) for step in offsets]
-    flags += [dom > 0, dom < lax.axis_size("dom") - 1, dom < 0, dom < 0]
-    flags = jnp.stack(flags).astype(F32).reshape(1, 8)
-
-    own, first, last = call(
-        trace_kernel,
-        (shaped(4, 8, SLOTS), shaped(4, RIM), shaped(4, RIM)),
-        4,
-        [(8, WIDE), (8 * TABS, LANES)],
-        us=5,
-    )(state, mesh_vel, disp, rows)
-    partners = [shift(own[k ^ 1], "group", -step) for k, step in enumerate(offsets)]
-    moved_before = shift(last, "dom", 1)
-    moved_after = shift(first, "dom", -1)
-
-    local, first, last = call(
-        element_kernel,
-        (shaped(8, WIDE), shaped(4, RIM), shaped(4, RIM)),
-        4,
-        [
-            (8, WIDE),
-            (6, 8 * ROWS, LANES),
-            (PA, 9, 15, 8, LANES),
-            (PA, 9, 12, 8, LANES),
-            (SLABS, 8, LANES),
+    base, terms = pl.pallas_call(
+        main_kernel,
+        out_shape=(shaped(8, WIDE), shaped(4, 8, SLOTS)),
+        in_specs=[HBM] * 7,
+        out_specs=(VMEM, VMEM),
+        scratch_shapes=[
+            pltpu.VMEM((1, 1), jnp.int32),
+            pltpu.VMEM((4, 1, CP), F32),
+            pltpu.VMEM((3, 1, CP), F32),
+            pltpu.VMEM((3, 1, CP), F32),
+            pltpu.VMEM((1, SLABS * SLOTS), F32),
+            pltpu.VMEM((4, SLOTS), jnp.int32),
+            pltpu.VMEM((4, SLOTS), F32),
+            pltpu.VMEM((8, WIDE), F32),
+            pltpu.VMEM((8, WIDE), F32),
+            pltpu.VMEM((6, 8 * ROWS, LANES), F32),
+            pltpu.VMEM((PA, 9, 15, 8, LANES), F32),
+            pltpu.VMEM((PA, 9, 12, 8, LANES), F32),
+            pltpu.VMEM((SLABS, 8, LANES), F32),
+            pltpu.VMEM((8 * TABS, LANES), F32),
+            pltpu.VMEM((8, RIM + LANES), F32),
+            pltpu.VMEM((4, 8, SLOTS), F32),
+            pltpu.VMEM((4, 8, SLOTS), F32),
+            pltpu.VMEM((4, 4, SLOTS), F32),
+            pltpu.VMEM((4, 4, SLOTS), F32),
+            pltpu.VMEM((2, 4, RIM), F32),
+            pltpu.VMEM((2, 4, RIM), F32),
+            pltpu.VMEM((2, 4, RIM), F32),
+            pltpu.VMEM((2, 4, RIM), F32),
+            pltpu.SemaphoreType.DMA((14,)),
+            pltpu.SemaphoreType.DMA((12,)),
+            pltpu.SemaphoreType.DMA((12,)),
         ],
-        scalars=(0,),
-        us=15,
-    )(live_slabs, state, mesh_vel, elem_size)
-    before = shift(last, "dom", 1)
-    after = shift(first, "dom", -1)
-    assembled, own2 = call(
-        assemble_kernel,
-        (shaped(8, WIDE), shaped(4, 4, SLOTS)),
-        4,
-        [(8, RIM + LANES), (8 * TABS, LANES)],
-        us=5,
-    )(local, before, after, rows)
-    reactions = [shift(own2[k ^ 1], "group", -step) for k, step in enumerate(offsets)]
-    residual, new_disp = call(
+        compiler_params=pltpu.CompilerParams(
+            vmem_limit_bytes=48 << 20, collective_id=0, has_side_effects=True
+        ),
+    )(live_slabs, state, mesh_vel, disp, elem_size, trace_rows, penalty)
+    return pl.pallas_call(
         finish_kernel,
-        (shaped(4, 1, CP), shaped(3, 1, CP)),
-        18,
-        [(8, WIDE), (8, WIDE), (8, RIM + LANES), (8, SLOTS)],
-        scalars=(0,),
-        us=8,
-    )(flags, assembled, mesh_vel, disp, rows, gammas, own, own2, *partners, *reactions, moved_before, moved_after)
-    return residual, new_disp
+        out_shape=(shaped(4, 1, CP), shaped(3, 1, CP)),
+        in_specs=[VMEM] * 3,
+        out_specs=(VMEM, VMEM),
+        scratch_shapes=[pltpu.VMEM((8, WIDE), F32)],
+        compiler_params=pltpu.CompilerParams(vmem_limit_bytes=16 << 20),
+    )(base, terms, rows)
 
 
 def solution(mesh):

time: 52.1 us -> 28.5 us (0.55)
  the two profiles are of different devices: /device:TPU:31 before, /device:TPU:0 now
where the time goes in v2:
time: 28.5 us; the launch traced here: 28 us
  Pallas kernels  21.9 us (77%)
  local copies, waits for them, and re-layouts  4.83 us (17%)
  between operations  1.3 us (5%)
    pallas_call x1, Pallas kernels, shards(): pl.pallas_call(main_kernel, out_shape=(shaped(8, WIDE), shaped(4, 8, SLOT...  20.1 us
    unnamed x12, local copies, waits for them, and re-layouts  4.83 us
    pallas_call x1, Pallas kernels, shards(): pl.pallas_call(finish_kernel, out_shape=(shaped(4, 1, CP), shaped(3, 1, C...  1.78 us

profile of v2, /device:TPU:0, one launch (start us, length us, event | category | flops | bytes accessed | tf_op | source)
XLA Modules:
  0.0 28.0 jit_solution(7808057104599776826)
XLA Ops:
  1.3 0.0 copy-start
  1.3 0.9 %copy-done = f32[4,1,7800]{2,1,0:T(1,128)S(1)} copy-done((f32[4,1,7800]{2,1,0:T(1,128)S(1)}, f32[4,1,7800]{2,1,0:T(1,128)}, u32[]{:S(2)}) %copy-start) | copy-done | bytes 124824
  2.2 0.0 copy-start.1
  2.2 0.9 %copy-done.1 = f32[3,1,7800]{2,1,0:T(1,128)S(1)} copy-done((f32[3,1,7800]{2,1,0:T(1,128)S(1)}, f32[3,1,7800]{2,1,0:T(1,128)}, u32[]{:S(2)}) %copy-start.1) | copy-done | bytes 93624
  3.1 0.0 copy-start.2
  3.1 0.9 %copy-done.2 = f32[3,1,7800]{2,1,0:T(1,128)S(1)} copy-done((f32[3,1,7800]{2,1,0:T(1,128)S(1)}, f32[3,1,7800]{2,1,0:T(1,128)}, u32[]{:S(2)}) %copy-start.2) | copy-done | bytes 93624
  4.0 0.0 copy-start.3
  4.0 0.7 %copy-done.3 = s32[1,1,4,1024]{3,2,1,0:T(4,128)S(1)} copy-done((s32[1,1,4,1024]{3,2,1,0:T(4,128)S(1)}, s32[1,1,4,1024]{3,2,1,0:T(4,128)}, u32[]{:S(2)}) %copy-start.3) | copy-done | bytes 16408
  4.7 0.0 copy-start.4
  4.7 0.7 %copy-done.4 = f32[1,4096]{1,0:T(1,128)S(1)} copy-done((f32[1,4096]{1,0:T(1,128)S(1)}, f32[1,4096]{1,0:T(1,128)}, u32[]{:S(2)}) %copy-start.4) | copy-done | bytes 16408
  5.4 0.0 copy-start.5
  5.4 0.7 %copy-done.5 = f32[1,1,4,1024]{3,2,1,0:T(4,128)S(1)} copy-done((f32[1,1,4,1024]{3,2,1,0:T(4,128)S(1)}, f32[1,1,4,1024]{3,2,1,0:T(4,128)}, u32[]{:S(2)}) %copy-start.5) | copy-done | bytes 16408
  6.1 20.1 %shard_map.86 = (f32[8,7936]{1,0:T(8,128)S(1)}, f32[4,8,1024]{2,1,0:T(8,128)S(1)}) custom-call(s32[1,1]{1,0:T(1,128)S(6)} %copy.9.live_hbm, f32[4,1,7800]{2,1,0:T(1,128)S(1)} %copy-done, f32[3,1,7800]{2,1,0:T(1,128)S(1)} %copy-done.1, f32[3,1,7800]{2,1,0:T(1,128)S(1)} %copy-done.2, f32[1,4096]{1,0:T(1,128)S(1)} %copy-done.4, ...), custom_call_target="tpu_custom_call" | custom-call | tf_op jit(solution)/shard_map/pallas_call | solution.py:545
  26.2 1.8 %shard_map.87 = (f32[4,1,7800]{2,1,0:T(1,128)}, f32[3,1,7800]{2,1,0:T(1,128)}) custom-call(f32[8,7936]{1,0:T(8,128)S(1)} %get-tuple-element.4.base_ref, f32[4,8,1024]{2,1,0:T(8,128)S(1)} %get-tuple-element.5.term_in_ref, s32[4,1024]{1,0:T(4,128)S(1)} %bitcast.1), custom_call_target="tpu_custom_call" | custom-call | tf_op jit(solution)/shard_map/pallas_call | solution.py:582
Async XLA Ops:
  1.3 0.9 %copy-start = (f32[4,1,7800]{2,1,0:T(1,128)S(1)}, f32[4,1,7800]{2,1,0:T(1,128)}, u32[]{:S(2)}) copy-start(f32[4,1,7800]{2,1,0:T(1,128)} %state_hbm.1) | copy-start | bytes 374404
  2.2 0.9 %copy-start.1 = (f32[3,1,7800]{2,1,0:T(1,128)S(1)}, f32[3,1,7800]{2,1,0:T(1,128)}, u32[]{:S(2)}) copy-start(f32[3,1,7800]{2,1,0:T(1,128)} %mesh_hbm.1) | copy-start | bytes 280804
  3.1 0.9 %copy-start.2 = (f32[3,1,7800]{2,1,0:T(1,128)S(1)}, f32[3,1,7800]{2,1,0:T(1,128)}, u32[]{:S(2)}) copy-start(f32[3,1,7800]{2,1,0:T(1,128)} %disp_hbm.1) | copy-start | bytes 280804
  4.0 0.7 %copy-start.3 = (s32[1,1,4,1024]{3,2,1,0:T(4,128)S(1)}, s32[1,1,4,1024]{3,2,1,0:T(4,128)}, u32[]{:S(2)}) copy-start(s32[1,1,4,1024]{3,2,1,0:T(4,128)} %rows_hbm.1) | copy-start | bytes 49156
  4.7 0.7 %copy-start.4 = (f32[1,4096]{1,0:T(1,128)S(1)}, f32[1,4096]{1,0:T(1,128)}, u32[]{:S(2)}) copy-start(f32[1,4096]{1,0:T(1,128)} %size_hbm.1) | copy-start | bytes 49156
  5.4 0.7 %copy-start.5 = (f32[1,1,4,1024]{3,2,1,0:T(4,128)S(1)}, f32[1,1,4,1024]{3,2,1,0:T(4,128)}, u32[]{:S(2)}) copy-start(f32[1,1,4,1024]{3,2,1,0:T(4,128)} %pen_hbm.1) | copy-start | bytes 49156

commit v3 on v2

--- a/solution.py
+++ b/solution.py
@@ -104,15 +104,19 @@
     return high, low
 
 
+def face_extra(x_ref):
+    lane = lane_iota()
+    extra = jnp.zeros((8, LANES), F32)
+    for k, flat in enumerate(EXTRAS):
+        extra = jnp.where(lane == k, x_ref[:, flat : flat + 1], extra)
+    return extra
+
+
 def face_tables(x_ref, tab_ref):
-    lane = lane_iota()
     for a in range(PA):
         tab_ref[16 * a : 16 * a + 8, :] = take_row(x_ref, a * PLANE)
         tab_ref[16 * a + 8 : 16 * a + 16, :] = take_row(x_ref, a * PLANE + 9 * PC)
-    extra = jnp.zeros((8, LANES), F32)
-    for k, flat in enumerate(EXTRAS):
-        extra = jnp.where(lane == k, x_ref[:, flat : flat + 1], extra)
-    tab_ref[96:104, :] = extra
+    tab_ref[96:104, :] = face_extra(x_ref)
     tab_ref[104:112, :] = jnp.zeros((8, LANES), F32)
     high, low = split_bf16(tab_ref[...])
     return jnp.concatenate([high, low], axis=0)
@@ -125,6 +129,57 @@
         piece = full[8 * h : 8 * h + 8] + full[112 + 8 * h : 120 + 8 * h]
         out = jnp.where(hi == h, piece, out)
     return out
+
+
+def low_half():
+    return lax.broadcasted_iota(jnp.int32, (8, LANES), 0) < 4
+
+
+def pair_tables(x_ref):
+    low = low_half()
+    tiles = []
+    for a in range(PA):
+        front = pltpu.roll(take_row(x_ref, a * PLANE), 4, 0)
+        tiles.append(jnp.where(low, front, take_row(x_ref, a * PLANE + 9 * PC)))
+    tiles.append(jnp.where(low, pltpu.roll(face_extra(x_ref), 4, 0), 0.0))
+    tiles.append(jnp.zeros((8, LANES), F32))
+    high, low = split_bf16(jnp.concatenate(tiles, axis=0))
+    return jnp.concatenate([high, low], axis=0)
+
+
+def paired(hi):
+    return hi - (lax.broadcasted_iota(jnp.int32, (8, SLOTS), 0) >= 4).astype(jnp.int32)
+
+
+def gather_pairs(table, hi, hot):
+    full = jnp.dot(table, hot, preferred_element_type=F32)
+    which = paired(hi)
+    out = jnp.zeros((8, SLOTS), F32)
+    for p in range(7):
+        piece = full[8 * p : 8 * p + 8] + full[64 + 8 * p : 72 + 8 * p]
+        out = jnp.where(which == 2 * p, piece, out)
+    return out[0:4] + out[4:8]
+
+
+def scatter_dot(term, which, step, tiles, hot):
+    high = term.astype(BF16).astype(F32)
+    low = term - high
+    spread = [jnp.where(which == step * p, high, 0.0) for p in range(tiles)]
+    spread += [jnp.where(which == step * p, low, 0.0) for p in range(tiles)]
+    lhs = jnp.concatenate(spread, axis=0).astype(BF16)
+    return lax.dot_general(lhs, hot, (((1,), (1,)), ((), ())), preferred_element_type=F32)
+
+
+def add_extra(d_ref, extra):
+    lane = lane_iota()
+    by_col = {}
+    for k, flat in enumerate(EXTRAS):
+        by_col.setdefault(flat // LANES, []).append((k, flat % LANES))
+    for col, entries in by_col.items():
+        val = d_ref[:, col * LANES : (col + 1) * LANES]
+        for k, at in entries:
+            val = val + jnp.where(lane == at, extra[:, k : k + 1], 0.0)
+        d_ref[:, col * LANES : (col + 1) * LANES] = val
 
 
 def fwd_value(x0, x1, x2):
@@ -196,7 +251,7 @@
                 acc_ref[a, q, k] = zero
         return carry
 
-    lax.fori_loop(0, PA, clear, 0)
+    lax.fori_loop(0, 2, clear, 0)
 
     def points(slab, q):
         h = h_ref[slab]
@@ -244,8 +299,9 @@
                 back_value(*coef_k[2][c]),
             )
             for k, part in enumerate(parts):
-                for s in range(3):
+                for s in range(2):
                     acc_ref[slab + s, q, 3 * c + k] += outer * part[s]
+                acc_ref[slab + 2, q, 3 * c + k] = outer * part[2]
 
     def slab_loop(slab, carry):
         def point_loop(q, inner):
@@ -256,12 +312,10 @@
 
     lax.fori_loop(0, SLABS, slab_loop, 0)
 
-    def clear_rows(r, carry):
+    for a in range(PA):
         for k in range(6):
-            q_ref[k, pl.ds(pl.multiple_of(r * 8, 8), 8), :] = zero
-        return carry
-
-    lax.fori_loop(0, ROWS, clear_rows, 0)
+            q_ref[k, a * 80 + 64 : a * 80 + 72, :] = zero
+            q_ref[k, a * 80 + 72 : a * 80 + 80, :] = zero
 
     def back_b(a, carry):
         for c in range(4):
@@ -271,7 +325,10 @@
                 ]
                 straight = both(pieces[0], pieces[1])
                 sloped = back_value(*pieces[2])
-                for s in range(3):
+                at = strided(a * 80 + 4 + c)
+                q_ref[qc, at, :] = straight[0]
+                q_ref[3 + qc, at, :] = sloped[0]
+                for s in range(1, 3):
                     at = strided(a * 80 + 8 * s + 4 + c)
                     q_ref[qc, at, :] += straight[s]
                     q_ref[3 + qc, at, :] += sloped[s]
@@ -313,11 +370,11 @@
 
 
 def main_kernel(
-    live_hbm, state_hbm, mesh_hbm, disp_hbm, size_hbm, rows_hbm, pen_hbm,
-    base_ref, term_ref,
-    live_ref, state_ref, mesh_ref, disp_ref, size_ref, rows_ref, pen_ref, x_ref, f_ref, q_ref, g_ref, acc_ref, h_ref, tab_ref, wide_ref,
+    live_ref, state_hbm, mesh_hbm, disp_hbm, size_hbm, rows_hbm, pen_hbm,
+    base_ref,
+    state_ref, mesh_ref, disp_ref, size_ref, rows_ref, pen_ref, x_ref, f_ref, q_ref, g_ref, acc_ref, h_ref, tab_ref, wide_ref,
     own_ref, part_ref, own2_ref, part2_ref, rim_ref, rim_in_ref, rim2_ref, rim2_in_ref,
-    load_sem, send_sem, recv_sem,
+    hot_ref, hi_ref, d_ref, term_ref, load_sem, send_sem, recv_sem,
 ):
     groups = lax.axis_size("group")
     doms = lax.axis_size("dom")
@@ -336,7 +393,6 @@
                 pltpu.make_async_copy(src.at[c], dst.at[c], load_sem.at[len(loads)])
             )
     small = (
-        (live_hbm, live_ref),
         (size_hbm, size_ref),
         (rows_hbm.at[0, 0], rows_ref),
         (pen_hbm.at[0, 0], pen_ref),
@@ -418,13 +474,16 @@
     table = face_tables(x_ref, tab_ref)
     for k in range(4):
         hi, lo = locate(rows_ref[k : k + 1, :])
-        own_ref[k] = gather_slots(table, hi, one_hot(lo))
+        hi_ref[k : k + 1, :] = hi
+        hot = one_hot(lo)
+        hot_ref[k] = hot
+        own_ref[k] = gather_slots(table, hi, hot)
 
     pl.semaphore_wait(barrier, peers)
     launch(rims)
     launch(traces)
 
-    live = jnp.broadcast_to(live_ref[...], (8, LANES))
+    live = jnp.zeros((8, LANES), jnp.int32) + live_ref[0, 0]
     element_stage(live, f_ref, q_ref, g_ref, acc_ref, h_ref, base_ref)
     cut_rims(base_ref, 4, rim2_ref)
     launch(rims2)
@@ -470,69 +529,59 @@
     for col in range(21):
         val = jnp.where(rim_cut(col), wide_ref[:, col * LANES : (col + 1) * LANES], 0.0)
         add_row(base_ref, LAST_COL * LANES + LAST_OFF + col * LANES, val)
-    table = face_tables(base_ref, tab_ref)
+    table = pair_tables(base_ref)
     for k in range(4):
-        hi, lo = locate(rows_ref[k : k + 1, :])
-        own2_ref[k] = gather_slots(table, hi, one_hot(lo))[4:8]
+        own2_ref[k] = gather_pairs(table, hi_ref[k : k + 1, :], hot_ref[k])
     launch(traces2)
 
+    d_ref[...] = jnp.zeros_like(d_ref)
     land(traces)
+    acc = jnp.zeros((2 * 8 * TABS, LANES), F32)
     for k, (_, _, present) in enumerate(slots):
         live_slot = present.astype(F32)
         gap = (part_ref[k] - own_ref[k]) * live_slot
-        term_ref[k] = gap
-        term_ref[k, 3:4, :] = jnp.zeros((1, SLOTS), F32) + live_slot
-        term_ref[k, 4:8, :] = -pen_ref[k : k + 1, :] * gap[4:8]
-    land(traces2)
-    for k, (_, _, present) in enumerate(slots):
-        half = 0.5 * present.astype(F32)
-        term_ref[k, 4:8, :] += half * (part2_ref[k] - own2_ref[k])
-    for copies in (rims, traces, rims2, traces2):
-        drain(copies)
-
-
-def finish_kernel(base_ref, term_in_ref, rows_ref, res_ref, new_ref, d_ref):
-    acc = jnp.zeros((2 * 8 * TABS, LANES), F32)
-    for k in range(4):
-        term = term_in_ref[k]
-        hi, lo = locate(rows_ref[k : k + 1, :])
-        hot = one_hot(lo)
-        high = term.astype(BF16).astype(F32)
-        low = term - high
-        spread = [jnp.where(hi == h, high, 0.0) for h in range(TABS)]
-        spread += [jnp.where(hi == h, low, 0.0) for h in range(TABS)]
-        lhs = jnp.concatenate(spread, axis=0).astype(BF16)
-        acc = acc + lax.dot_general(
-            lhs, hot, (((1,), (1,)), ((), ())), preferred_element_type=F32
-        )
+        term_ref[...] = gap
+        term_ref[3:4, :] = jnp.zeros((1, SLOTS), F32) + live_slot
+        term_ref[4:8, :] = -pen_ref[k : k + 1, :] * gap[4:8] - (0.5 * live_slot) * own2_ref[k]
+        acc = acc + scatter_dot(term_ref[...], hi_ref[k : k + 1, :], 1, TABS, hot_ref[k])
     sums = acc[: 8 * TABS] + acc[8 * TABS :]
-    d_ref[...] = jnp.zeros_like(d_ref)
     for a in range(PA):
         add_row(d_ref, a * PLANE, sums[16 * a : 16 * a + 8])
         add_row(d_ref, a * PLANE + 9 * PC, sums[16 * a + 8 : 16 * a + 16])
-    lane = lane_iota()
-    extra = sums[96:104]
-    by_col = {}
-    for k, flat in enumerate(EXTRAS):
-        by_col.setdefault(flat // LANES, []).append((k, flat % LANES))
-    for col, entries in by_col.items():
-        val = d_ref[:, col * LANES : (col + 1) * LANES]
-        for k, at in entries:
-            val = val + jnp.where(lane == at, extra[:, k : k + 1], 0.0)
-        d_ref[:, col * LANES : (col + 1) * LANES] = val
-    top = lax.broadcasted_iota(jnp.int32, (8, LANES), 0) < 3
+    add_extra(d_ref, sums[96:104])
     for col in range(COLS):
         cut = slice(col * LANES, (col + 1) * LANES)
         d = d_ref[:, cut]
         averaged = d / (2.0 * jnp.maximum(d[3:4], 1.0))
-        d_ref[:, cut] = jnp.where(top, averaged, d) + base_ref[:, cut]
+        base_ref[:, cut] += jnp.where(top, averaged, d)
+
+    land(traces2)
+    acc = jnp.zeros((128, LANES), F32)
+    for k, (_, _, present) in enumerate(slots):
+        half = (0.5 * present.astype(F32)) * part2_ref[k]
+        term_ref[0:4, :] = half
+        term_ref[4:8, :] = half
+        acc = acc + scatter_dot(term_ref[...], paired(hi_ref[k : k + 1, :]), 2, 8, hot_ref[k])
+    sums = acc[:64] + acc[64:]
+    low = low_half()
+    for a in range(PA):
+        tile = sums[8 * a : 8 * a + 8]
+        add_row(base_ref, a * PLANE, jnp.where(low, 0.0, pltpu.roll(tile, 4, 0)))
+        add_row(base_ref, a * PLANE + 9 * PC, jnp.where(low, 0.0, tile))
+    add_extra(base_ref, jnp.where(low, 0.0, pltpu.roll(sums[48:56], 4, 0)))
+    for copies in (rims, traces, rims2, traces2):
+        drain(copies)
+
+
+def finish_kernel(base_ref, res_ref, new_ref):
     for c in range(3):
-        new_ref[c] = d_ref[c : c + 1, :CP]
+        new_ref[c] = base_ref[c : c + 1, :CP]
     for c in range(4):
-        res_ref[c] = d_ref[4 + c : 5 + c, :CP]
+        res_ref[c] = base_ref[4 + c : 5 + c, :CP]
 
 
 VMEM = pl.BlockSpec(memory_space=pltpu.VMEM)
+SMEM = pl.BlockSpec(memory_space=pltpu.SMEM)
 HBM = pl.BlockSpec(memory_space=pltpu.HBM)
 
 
@@ -541,14 +590,12 @@
 
 
 def shards(state, mesh_vel, disp, elem_size, live_slabs, trace_rows, penalty):
-    rows = trace_rows.reshape(4, SLOTS)
-    base, terms = pl.pallas_call(
+    base = pl.pallas_call(
         main_kernel,
-        out_shape=(shaped(8, WIDE), shaped(4, 8, SLOTS)),
-        in_specs=[HBM] * 7,
-        out_specs=(VMEM, VMEM),
+        out_shape=shaped(8, WIDE),
+        in_specs=[SMEM] + [HBM] * 6,
+        out_specs=VMEM,
         scratch_shapes=[
-            pltpu.VMEM((1, 1), jnp.int32),
             pltpu.VMEM((4, 1, CP), F32),
             pltpu.VMEM((3, 1, CP), F32),
             pltpu.VMEM((3, 1, CP), F32),
@@ -571,22 +618,25 @@
             pltpu.VMEM((2, 4, RIM), F32),
             pltpu.VMEM((2, 4, RIM), F32),
             pltpu.VMEM((2, 4, RIM), F32),
-            pltpu.SemaphoreType.DMA((14,)),
+            pltpu.VMEM((4, LANES, SLOTS), BF16),
+            pltpu.VMEM((4, SLOTS), jnp.int32),
+            pltpu.VMEM((8, WIDE), F32),
+            pltpu.VMEM((8, SLOTS), F32),
+            pltpu.SemaphoreType.DMA((13,)),
             pltpu.SemaphoreType.DMA((12,)),
             pltpu.SemaphoreType.DMA((12,)),
         ],
         compiler_params=pltpu.CompilerParams(
             vmem_limit_bytes=48 << 20, collective_id=0, has_side_effects=True
         ),
-    )(live_slabs, state, mesh_vel, disp, elem_size, trace_rows, penalty)
+    )(live_slabs, *[pltpu.with_memory_space_constraint(x, pltpu.HBM) for x in (state, mesh_vel, disp, elem_size, trace_rows, penalty)])
     return pl.pallas_call(
         finish_kernel,
         out_shape=(shaped(4, 1, CP), shaped(3, 1, CP)),
-        in_specs=[VMEM] * 3,
+        in_specs=[VMEM],
         out_specs=(VMEM, VMEM),
-        scratch_shapes=[pltpu.VMEM((8, WIDE), F32)],
         compiler_params=pltpu.CompilerParams(vmem_limit_bytes=16 << 20),
-    )(base, terms, rows)
+    )(base)
 
 
 def solution(mesh):

time: 28.5 us -> 22.8 us (0.80); the launches traced: 28 us -> 22.6 us
  local copies, waits for them, and re-layouts: 4.83 us -> 0 us
  Pallas kernels: 21.9 us -> 21.4 us
    unnamed x12 -> x0, local copies, waits for them, and re-layouts: 4.83 us -> none
    pallas_call x1, Pallas kernels: 1.78 us -> 0.72 us  [shards(): pl.pallas_call(finish_kernel, out_shape=(shaped(4, 1, CP), shaped(3, 1, C...]
    pallas_call x1, Pallas kernels: 20.1 us -> 20.6 us  [shards(): pl.pallas_call(main_kernel, out_shape=shaped(8, WIDE), in_specs=[SMEM] +...]
where the time goes in v3:
time: 22.8 us; the launch traced here: 22.6 us
  Pallas kernels  21.4 us (94%)
  between operations  1.29 us (6%)
    pallas_call x1, Pallas kernels, shards(): pl.pallas_call(main_kernel, out_shape=shaped(8, WIDE), in_specs=[SMEM] +...  20.6 us
    pallas_call x1, Pallas kernels, shards(): pl.pallas_call(finish_kernel, out_shape=(shaped(4, 1, CP), shaped(3, 1, C...  0.72 us

profile of v3, /device:TPU:0, one launch (start us, length us, event | category | flops | bytes accessed | tf_op | source)
XLA Modules:
  0.0 22.6 jit_solution(3327341237373105692)
XLA Ops:
  1.3 20.6 %shard_map.86.base_ref = f32[8,7936]{1,0:T(8,128)S(1)} custom-call(s32[1,1]{1,0:T(1,128)S(6)} %copy.9.live_ref, f32[4,1,7800]{2,1,0:T(1,128)} %state_hbm.1, f32[3,1,7800]{2,1,0:T(1,128)} %mesh_hbm.1, f32[3,1,7800]{2,1,0:T(1,128)} %disp_hbm.1, f32[1,4096]{1,0:T(1,128)} %size_hbm.1, s32[1,1,4,1024]{3,2,1,0:T(4,128)} %rows_hbm.1, f32[1,1,4,1024]{3,2,1,0:T(4,128)} %pen_hbm.1), custom_call_target="tpu_custom_call" | custom-call | tf_op jit(solution)/shard_map/pallas_call | solution.py:593
  21.9 0.7 %shard_map.87 = (f32[4,1,7800]{2,1,0:T(1,128)}, f32[3,1,7800]{2,1,0:T(1,128)}) custom-call(f32[8,7936]{1,0:T(8,128)S(1)} %shard_map.86.base_ref), custom_call_target="tpu_custom_call" | custom-call | tf_op jit(solution)/shard_map/pallas_call | solution.py:633

commit v4 on v3

--- a/solution.py
+++ b/solution.py
@@ -304,11 +304,12 @@
                 acc_ref[slab + 2, q, 3 * c + k] = outer * part[2]
 
     def slab_loop(slab, carry):
-        def point_loop(q, inner):
-            points(slab, q)
+        def point_loop(i, inner):
+            for k in range(3):
+                points(slab, 3 * i + k)
             return inner
 
-        return lax.fori_loop(0, 9, point_loop, carry)
+        return lax.fori_loop(0, 3, point_loop, carry)
 
     lax.fori_loop(0, SLABS, slab_loop, 0)
 
@@ -456,21 +457,32 @@
     rims = exchange(rim_ref, rim_in_ref, sides, 8)
     rims2 = exchange(rim2_ref, rim2_in_ref, sides, 10)
 
-    for load in loads:
+    for load in loads[:7] + loads[10:11]:
+        load.wait()
+    for c in range(3):
+        f_ref[4 + c : 5 + c, :CP] = state_ref[c] - mesh_ref[c]
+    f_ref[7:8, :CP] = jnp.zeros((1, CP), F32)
+    for c in range(4):
+        f_ref[c : c + 1, :CP] = state_ref[c]
+    f_ref[:, COLS * LANES :] = jnp.zeros((8, LANES), F32)
+    for k in range(32):
+        h_ref[k // 8, k % 8 : k % 8 + 1, :] = size_ref[:, k * LANES : (k + 1) * LANES]
+    live = jnp.zeros((8, LANES), jnp.int32) + live_ref[0, 0]
+    element_stage(live, f_ref, q_ref, g_ref, acc_ref, h_ref, base_ref)
+    cut_rims(base_ref, 4, rim2_ref)
+    pl.semaphore_wait(barrier, peers)
+    launch(rims2)
+
+    for load in loads[7:10] + loads[11:]:
         load.wait()
     for c in range(3):
         x_ref[c : c + 1, :CP] = disp_ref[c] + 0.5 * mesh_ref[c]
-        f_ref[4 + c : 5 + c, :CP] = state_ref[c] - mesh_ref[c]
     x_ref[3:4, :CP] = jnp.zeros((1, CP), F32)
-    f_ref[7:8, :CP] = jnp.zeros((1, CP), F32)
     for c in range(4):
         x_ref[4 + c : 5 + c, :CP] = state_ref[c]
-        f_ref[c : c + 1, :CP] = state_ref[c]
     x_ref[:, COLS * LANES :] = jnp.zeros((8, LANES), F32)
-    f_ref[:, COLS * LANES :] = jnp.zeros((8, LANES), F32)
-    for k in range(32):
-        h_ref[k // 8, k % 8 : k % 8 + 1, :] = size_ref[:, k * LANES : (k + 1) * LANES]
     cut_rims(x_ref, 0, rim_ref)
+    launch(rims)
     table = face_tables(x_ref, tab_ref)
     for k in range(4):
         hi, lo = locate(rows_ref[k : k + 1, :])
@@ -478,15 +490,7 @@
         hot = one_hot(lo)
         hot_ref[k] = hot
         own_ref[k] = gather_slots(table, hi, hot)
-
-    pl.semaphore_wait(barrier, peers)
-    launch(rims)
     launch(traces)
-
-    live = jnp.zeros((8, LANES), jnp.int32) + live_ref[0, 0]
-    element_stage(live, f_ref, q_ref, g_ref, acc_ref, h_ref, base_ref)
-    cut_rims(base_ref, 4, rim2_ref)
-    launch(rims2)
 
     for k, (_, _, present) in enumerate(slots):
 
@@ -501,24 +505,6 @@
         def _():
             rim_in_ref[k] = jnp.zeros((4, RIM), F32)
             rim2_in_ref[k] = jnp.zeros((4, RIM), F32)
-
-    land(rims)
-    has_prev = 0.5 * sides[0][2].astype(F32)
-    has_next = 0.5 * sides[1][2].astype(F32)
-    top = lax.broadcasted_iota(jnp.int32, (8, LANES), 0) < 3
-    for col in range(COLS):
-        cut = slice(col * LANES, (col + 1) * LANES)
-        base_ref[:, cut] = jnp.where(top, x_ref[:, cut], base_ref[:, cut])
-    widen(rim_in_ref.at[0], wide_ref, 0)
-    for col in range(21):
-        cut = slice(col * LANES, (col + 1) * LANES)
-        val = take_row(wide_ref, LAST_OFF + col * LANES) - x_ref[:, cut]
-        base_ref[:, cut] += jnp.where(rim_cut(col) & top, has_prev * val, 0.0)
-    widen(rim_in_ref.at[1], wide_ref, 0)
-    for col in range(21):
-        start = LAST_COL * LANES + LAST_OFF + col * LANES
-        val = wide_ref[:, col * LANES : (col + 1) * LANES] - take_row(x_ref, start)
-        add_row(base_ref, start, jnp.where(rim_cut(col) & top, has_next * val, 0.0))
 
     land(rims2)
     widen(rim2_in_ref.at[0], wide_ref, 4)
@@ -535,6 +521,23 @@
     launch(traces2)
 
     d_ref[...] = jnp.zeros_like(d_ref)
+    top = lax.broadcasted_iota(jnp.int32, (8, LANES), 0) < 3
+    for col in range(COLS):
+        cut = slice(col * LANES, (col + 1) * LANES)
+        base_ref[:, cut] = jnp.where(top, x_ref[:, cut], base_ref[:, cut])
+    land(rims)
+    has_prev = 0.5 * sides[0][2].astype(F32)
+    has_next = 0.5 * sides[1][2].astype(F32)
+    widen(rim_in_ref.at[0], wide_ref, 0)
+    for col in range(21):
+        cut = slice(col * LANES, (col + 1) * LANES)
+        val = take_row(wide_ref, LAST_OFF + col * LANES) - x_ref[:, cut]
+        base_ref[:, cut] += jnp.where(rim_cut(col) & top, has_prev * val, 0.0)
+    widen(rim_in_ref.at[1], wide_ref, 0)
+    for col in range(21):
+        start = LAST_COL * LANES + LAST_OFF + col * LANES
+        val = wide_ref[:, col * LANES : (col + 1) * LANES] - take_row(x_ref, start)
+        add_row(base_ref, start, jnp.where(rim_cut(col) & top, has_next * val, 0.0))
     land(traces)
     acc = jnp.zeros((2 * 8 * TABS, LANES), F32)
     for k, (_, _, present) in enumerate(slots):

time: 22.8 us -> 21.7 us (0.952)
  Pallas kernels: 21.4 us -> 20.2 us
    pallas_call x1, Pallas kernels: 20.6 us -> 19.5 us  [shards(): pl.pallas_call(main_kernel, out_shape=shaped(8, WIDE), in_specs=[SMEM] +...]
where the time goes in v4:
time: 21.7 us; the launch traced here: 21.5 us
  Pallas kernels  20.2 us (93%)
  between operations  1.29 us (6%)
    pallas_call x1, Pallas kernels, shards(): pl.pallas_call(main_kernel, out_shape=shaped(8, WIDE), in_specs=[SMEM] +...  19.5 us
    pallas_call x1, Pallas kernels, shards(): pl.pallas_call(finish_kernel, out_shape=(shaped(4, 1, CP), shaped(3, 1, C...  0.72 us

profile of v4, /device:TPU:0, one launch (start us, length us, event | category | flops | bytes accessed | tf_op | source)
XLA Modules:
  0.0 21.5 jit_solution(3468393812826880423)
XLA Ops:
  1.3 19.5 %shard_map.86.base_ref = f32[8,7936]{1,0:T(8,128)S(1)} custom-call(s32[1,1]{1,0:T(1,128)S(6)} %copy.9.live_ref, f32[4,1,7800]{2,1,0:T(1,128)} %state_hbm.1, f32[3,1,7800]{2,1,0:T(1,128)} %mesh_hbm.1, f32[3,1,7800]{2,1,0:T(1,128)} %disp_hbm.1, f32[1,4096]{1,0:T(1,128)} %size_hbm.1, s32[1,1,4,1024]{3,2,1,0:T(4,128)} %rows_hbm.1, f32[1,1,4,1024]{3,2,1,0:T(4,128)} %pen_hbm.1), custom_call_target="tpu_custom_call" | custom-call | tf_op jit(solution)/shard_map/pallas_call | solution.py:596
  20.8 0.7 %shard_map.87 = (f32[4,1,7800]{2,1,0:T(1,128)}, f32[3,1,7800]{2,1,0:T(1,128)}) custom-call(f32[8,7936]{1,0:T(8,128)S(1)} %shard_map.86.base_ref), custom_call_target="tpu_custom_call" | custom-call | tf_op jit(solution)/shard_map/pallas_call | solution.py:636

commit v5 on v4

--- a/solution.py
+++ b/solution.py
@@ -341,17 +341,15 @@
     pending = zero
     for r in range(ROWS):
         y = [q_ref[k, 8 * r : 8 * r + 8, :] for k in range(6)]
-        y0, y1, y2 = both(y[:3], y[3:])
-        y1 = pltpu.roll(y1, 1, 1)
-        y2 = pltpu.roll(y2, 2, 1)
-        main = y0 + jnp.where(lane >= 1, y1, 0.0) + jnp.where(lane >= 2, y2, 0.0)
-        tail = jnp.where(lane < 1, y1, 0.0) + jnp.where(lane < 2, y2, 0.0)
-        off = 2 * r
-        if off:
-            main = pltpu.roll(main, off, 1)
-            tail = pltpu.roll(tail, off, 1)
-        out_ref[:, r * LANES : (r + 1) * LANES] = jnp.where(lane >= off, main, pending)
-        pending = jnp.where(lane < off, main, tail)
+        column, following = pending, zero
+        for k, val in enumerate(both(y[:3], y[3:])):
+            off = 2 * r + k
+            if off:
+                val = pltpu.roll(val, off, 1)
+            column = column + jnp.where(lane >= off, val, 0.0)
+            following = following + jnp.where(lane < off, val, 0.0)
+        out_ref[:, r * LANES : (r + 1) * LANES] = column
+        pending = following
     out_ref[:, ROWS * LANES : (ROWS + 1) * LANES] = pending
     out_ref[:, COLS * LANES :] = zero
 

time: 21.7 us -> 20.1 us (0.926)
  Pallas kernels: 20.2 us -> 18.6 us
    pallas_call x1, Pallas kernels: 19.5 us -> 17.8 us  [shards(): pl.pallas_call(main_kernel, out_shape=shaped(8, WIDE), in_specs=[SMEM] +...]
where the time goes in v5:
time: 20.1 us; the launch traced here: 19.9 us
  Pallas kernels  18.6 us (93%)
  between operations  1.29 us (6%)
    pallas_call x1, Pallas kernels, shards(): pl.pallas_call(main_kernel, out_shape=shaped(8, WIDE), in_specs=[SMEM] +...  17.8 us
    pallas_call x1, Pallas kernels, shards(): pl.pallas_call(finish_kernel, out_shape=(shaped(4, 1, CP), shaped(3, 1, C...  0.72 us

profile of v5, /device:TPU:0, one launch (start us, length us, event | category | flops | bytes accessed | tf_op | source)
XLA Modules:
  0.0 19.9 jit_solution(9195324088428076213)
XLA Ops:
  1.3 17.8 %shard_map.86.base_ref = f32[8,7936]{1,0:T(8,128)S(1)} custom-call(s32[1,1]{1,0:T(1,128)S(6)} %copy.9.live_ref, f32[4,1,7800]{2,1,0:T(1,128)} %state_hbm.1, f32[3,1,7800]{2,1,0:T(1,128)} %mesh_hbm.1, f32[3,1,7800]{2,1,0:T(1,128)} %disp_hbm.1, f32[1,4096]{1,0:T(1,128)} %size_hbm.1, s32[1,1,4,1024]{3,2,1,0:T(4,128)} %rows_hbm.1, f32[1,1,4,1024]{3,2,1,0:T(4,128)} %pen_hbm.1), custom_call_target="tpu_custom_call" | custom-call | tf_op jit(solution)/shard_map/pallas_call | solution.py:594
  19.1 0.7 %shard_map.87 = (f32[4,1,7800]{2,1,0:T(1,128)}, f32[3,1,7800]{2,1,0:T(1,128)}) custom-call(f32[8,7936]{1,0:T(8,128)S(1)} %shard_map.86.base_ref), custom_call_target="tpu_custom_call" | custom-call | tf_op jit(solution)/shard_map/pallas_call | solution.py:634
